TPU v7x, 32 devices: a whole 2x2x4 slice. The times are simulated.
32 devices in a mesh: row: 2 (over y), col: 4 (over z), layer: 4 (over x, core).
Axes of the slice: x: 2, y: 2, z: 4, core: 2. Of those that a mesh axis runs over, the one named last changes fastest.
Arguments:
- eigvecs: float32 [16384, 8192], P('row', ('col', 'layer')), may hold values from -6 to 6
- first_vectors: float32 [16384, 128], P(('row', 'layer'), 'col'), may hold values from -0.375 to 0.375
- second_vectors: float32 [16384, 128], P(('row', 'layer'), 'col'), may hold values from -0.375 to 0.375
- first_factors: float32 [8192, 128], P(('row', 'layer'), 'col'), may hold values from -0.5 to 0.5
- second_factors: float32 [8192, 128], P(('row', 'layer'), 'col'), may hold values from -0.5 to 0.5
- panel_vectors: float32 [16384, 256], P(('row', 'layer')), may hold values from -0.125 to 0.125
- panel_factor: float32 [256, 256], replicated, may hold values from -0.375 to 0.375
Outputs:
- transformed: float32 [16384, 8192], P(('row', 'layer'), 'col')
All inputs are finite; a program needn't handle non-finite values.
Results may differ from a plain program's by a relative error of at most 0.000082.
Values sent between devices are 32-bit elements; how exact they have to be, the bound alone decides.
No kernel may reach another device: no remote copies, remote signals or barrier semaphores. Data moves between devices by JAX's collectives and lax.ppermute only.
A program may use at most 128 MiB of HBM per device.

v0:
```python
import functools

import jax
import jax.numpy as jnp
from jax import lax
from jax.experimental import pallas as pl
from jax.experimental.pallas import tpu as pltpu
from jax.sharding import PartitionSpec as P


WIN = 256
HALF = 128
LANE = 128
F32 = jnp.float32
BF16 = jnp.bfloat16


def split(value):
    high = value.astype(BF16)
    return high, (value - high.astype(F32)).astype(BF16)


def dot(a, b):
    return jnp.dot(a, b, preferred_element_type=F32)


def product(a_high, a_low, b):
    b_high, b_low = split(b)
    return dot(a_high, b_high) + (dot(a_high, b_low) + dot(a_low, b_high))


def window_matrix(vec_t, fac_t):
    rows = lax.broadcasted_iota(jnp.int32, fac_t.shape, 0)
    cols = lax.broadcasted_iota(jnp.int32, fac_t.shape, 1)
    upper = jnp.where(rows >= cols, fac_t, 0.0).T
    up_high, up_low = split(upper)
    scaled = product(up_high, up_low, vec_t)
    v_high, v_low = split(vec_t.T)
    return product(v_high, v_low, scaled)


def params(*names):
    return pltpu.CompilerParams(dimension_semantics=names)


def cost(flops, size):
    return pl.CostEstimate(flops=flops, bytes_accessed=size, transcendentals=0)


def fill(place, shards, parts, store):
    own, mate = parts[:shards], parts[shards : 2 * shards]
    for s in range(shards):
        size = own[s].shape[0]
        source = lax.rem(place[2] - s + shards, shards)
        at = pl.ds(pl.multiple_of(source * size, 8), size)
        store[place[1], at, :] = own[s][...]
        store[1 - place[1], at, :] = mate[s][...]


def edge_matrices_kernel(shards, place, *refs):
    high, low, edges = refs[2 * shards :]

    @pl.when(pl.program_id(0) == 0)
    def _():
        fill(place, shards, refs, edges)

    base = pl.program_id(0) * 5 * HALF

    def edge(side, start, size):
        return edges[side, :, pl.ds(pl.multiple_of(base + start, LANE), size)]

    above = window_matrix(edge(1, 0, WIN), edge(1, 3 * HALF, HALF))
    below = window_matrix(edge(0, 0, WIN), edge(0, 3 * HALF, HALF))
    middle = jnp.concatenate([edge(1, WIN, HALF), edge(0, WIN, HALF)], axis=1)
    middle = window_matrix(middle, edge(0, 4 * HALF, HALF))
    for i, value in enumerate((above, below, middle)):
        h, l = split(value)
        high[0, i] = h
        low[0, i] = l


def edge_matrices(place, own, mate):
    shards = len(own)
    house, width = shards * own[0].shape[0], own[0].shape[1]
    edge = pl.BlockSpec((1, 3, WIN, WIN), lambda k, place: (k, 0, 0, 0))
    shape = jax.ShapeDtypeStruct((3, 3, WIN, WIN), BF16)
    return pl.pallas_call(
        functools.partial(edge_matrices_kernel, shards),
        out_shape=(shape, shape),
        grid_spec=pltpu.PrefetchScalarGridSpec(
            num_scalar_prefetch=1,
            grid=(3,),
            in_specs=[pl.BlockSpec(a.shape, lambda k, place: (0, 0)) for a in (*own, *mate)],
            out_specs=[edge, edge],
            scratch_shapes=[pltpu.VMEM((2, house, width), F32)],
        ),
        compiler_params=params("arbitrary"),
        cost_estimate=cost(2 * 10**9, 4 * 2**20),
        name="edge_matrices",
    )(place, *own, *mate)


def matrices_kernel(nt, group, shards, place, *refs):
    panel, panel_mate, mats, vecs = refs[2 * shards :]
    rows = nt * WIN

    @pl.when(pl.program_id(0) == 0)
    def _():
        fill(place, shards, refs, vecs)

    def piece(tile, start, size):
        return vecs[tile, :, pl.ds(pl.multiple_of(start, LANE), size)]

    for i in range(group):
        k = pl.program_id(0) * group + i
        tile = k // nt
        at = k % nt
        factor = piece(tile, 2 * rows + at * HALF, HALF)
        h, l = split(window_matrix(piece(tile, at * WIN, WIN), factor))
        mats[i, 0] = h
        mats[i, 1] = l
        before = jnp.maximum(k * WIN - HALF, 0)
        left = piece(before // rows, rows + before % rows, HALF)
        right = piece(tile, rows + at * WIN, HALF)
        factor = piece(tile, 2 * rows + rows // 2 + at * HALF, HALF)
        h, l = split(window_matrix(jnp.concatenate([left, right], axis=1), factor))
        mats[i, 2] = h
        mats[i, 3] = l
        block = slice(i * WIN, (i + 1) * WIN)
        mine = tile == place[1]
        h, l = split(jnp.where(mine, panel[block, :], panel_mate[block, :]).T)
        mats[i, 4] = h
        mats[i, 5] = l


def window_matrices(place, own, mate, panel, panel_mate, nt):
    shards = len(own)
    nw = 2 * nt
    group = 2
    arrays = (*own, *mate)
    in_specs = [pl.BlockSpec(a.shape, lambda k, place: (0, 0)) for a in arrays]
    width = panel.shape[1]
    panel_spec = pl.BlockSpec((group * WIN, width), lambda k, place: (k % (nt // group), 0))
    house = shards * own[0].shape[0]
    return pl.pallas_call(
        functools.partial(matrices_kernel, nt, group, shards),
        out_shape=jax.ShapeDtypeStruct((nw, 6, WIN, WIN), BF16),
        grid_spec=pltpu.PrefetchScalarGridSpec(
            num_scalar_prefetch=1,
            grid=(nw // group,),
            in_specs=[*in_specs, panel_spec, panel_spec],
            out_specs=pl.BlockSpec((group, 6, WIN, WIN), lambda k, place: (k, 0, 0, 0)),
            scratch_shapes=[pltpu.VMEM((2, house, own[0].shape[1]), F32)],
        ),
        compiler_params=params("arbitrary"),
        cost_estimate=cost(6 * 10**9, 24 * 2**20),
        name="window_matrices",
    )(place, *arrays, panel, panel_mate)


def edge_kernel(high, low, above, below, out):
    a = above[0]
    b = below[0]
    a = a - product(high[0, 0], low[0, 0], a)
    b = b - product(high[0, 1], low[0, 1], b)
    m = jnp.concatenate([a[HALF:], b[:HALF]], axis=0)
    m = m - product(high[0, 2], low[0, 2], m)
    out[0, 0, :HALF] = a[:HALF]
    out[0, 0, HALF:] = m[:HALF]
    out[0, 1, :HALF] = m[HALF:]
    out[0, 1, HALF:] = b[HALF:]


def sweep_edges(high, low, above, below):
    width = above.shape[2]
    mats = pl.BlockSpec((1, 3, WIN, WIN), lambda b, i: (b, 0, 0, 0))
    step = min(width, 2 * LANE)
    data = pl.BlockSpec((1, WIN, step), lambda b, i: (b, 0, i))
    return pl.pallas_call(
        edge_kernel,
        out_shape=jax.ShapeDtypeStruct((3, 2, WIN, width), F32),
        grid=(3, width // step),
        in_specs=[mats, mats, data, data],
        out_specs=pl.BlockSpec((1, 2, WIN, step), lambda b, i: (b, 0, 0, i)),
        compiler_params=params("arbitrary", "arbitrary"),
        cost_estimate=cost(6 * 10**9, 8 * 2**20),
        name="sweep_edges",
    )(high, low, above, below)


def stacked_product(mats, k, at, data):
    high, low = split(data)
    left = jnp.concatenate([mats[k, at], mats[k, at], mats[k, at + 1]], axis=1)
    return dot(left, jnp.concatenate([high, low, high], axis=0))


def sweep_kernel(nt, first, count, place, *refs):
    data, own_edge, recv_edge, mats_in = refs[:4]
    recv = refs[4 : 4 + count]
    keep, send, part, data_buf, mats, data_sems, mats_sems, out_sems = refs[4 + count :]
    nw = 2 * nt
    x, core = place[0], place[1]
    width = count * LANE
    own_at = pl.ds(pl.multiple_of(x * width, LANE), width)
    columns = pl.ds(first * LANE, width)

    def block(k):
        return pl.ds(pl.multiple_of(k * WIN, WIN), WIN)

    def received(i):
        return pl.ds(pl.multiple_of((1 - x) * width + i * LANE, LANE), LANE)

    def mats_copy(k):
        return pltpu.make_async_copy(mats_in.at[k], mats.at[k], mats_sems.at[k])

    def inner_copies(k):
        found = [
            pltpu.make_async_copy(
                data.at[block(x * nw + k), columns], data_buf.at[block(k), own_at], data_sems.at[k, 0]
            )
        ]
        for i in range(count):
            found.append(
                pltpu.make_async_copy(
                    recv[i].at[block(k - 1), :],
                    data_buf.at[block(k), received(i)],
                    data_sems.at[k, 1 + i],
                )
            )
        return found

    def edge_copies(end):
        k = end * (nw - 1)
        other_at = pl.ds(pl.multiple_of((1 - x) * width, LANE), width)
        return [
            pltpu.make_async_copy(
                own_edge.at[x + end, 1 - end, :, columns],
                data_buf.at[block(k), own_at],
                data_sems.at[k, 0],
            ),
            pltpu.make_async_copy(
                recv_edge.at[end, :, columns], data_buf.at[block(k), other_at], data_sems.at[k, 1]
            ),
        ]

    def out_copy(ref, b, tile):
        return pltpu.make_async_copy(
            data_buf.at[block(b), :], ref.at[block(b - tile * nt), :], out_sems.at[b]
        )

    for copy in edge_copies(0):
        copy.start()
    mats_copy(0).start()

    @pl.loop(1, nw - 1)
    def _(k):
        for copy in inner_copies(k):
            copy.start()
        mats_copy(k).start()

    for copy in edge_copies(1):
        copy.start()
    mats_copy(nw - 1).start()
    part[...] = jnp.zeros_like(part)
    for copy in edge_copies(0):
        copy.wait()
    mats_copy(0).wait()

    def stage(t, one, two, three):
        if one:
            for copy in inner_copies(t):
                copy.wait()
            mats_copy(t).wait()
        elif two and three:
            if isinstance(t, int) and t == nw - 1:
                for copy in edge_copies(1):
                    copy.wait()
                mats_copy(nw - 1).wait()
        r1 = block(t)
        r2 = pl.ds(pl.multiple_of((t - 1) * WIN - HALF, HALF), WIN)
        b = t - 3
        r3 = block(b)
        d1 = data_buf[r1, :] if one else None
        d2 = data_buf[r2, :] if two else None
        d3 = data_buf[r3, :] if three else None
        if one:
            d1 = d1 - stacked_product(mats, t, 0, d1)
        if two:
            d2 = d2 - stacked_product(mats, t - 1, 2, d2)
        if three:
            d3 = stacked_product(mats, b, 4, d3)
        if one:
            data_buf[r1, :] = d1
        if two:
            data_buf[r2, :] = d2
        if three:
            part[...] += d3
            mine = b // nt == core

            @pl.when(mine)
            def _():
                out_copy(keep, b, core).start()

            @pl.when(jnp.logical_not(mine))
            def _():
                out_copy(send, b, 1 - core).start()

    stage(1, True, False, False)
    stage(2, True, True, False)

    @pl.loop(3, nw - 1)
    def _(t):
        stage(t, True, True, True)

    stage(nw - 1, False, True, True)
    stage(nw, False, True, True)
    stage(nw + 1, False, False, True)
    stage(nw + 2, False, False, True)

    @pl.loop(0, nt)
    def _(i):
        out_copy(keep, core * nt + i, core).wait()
        out_copy(send, (1 - core) * nt + i, 1 - core).wait()


def sweep_chunk(place, first, data, recv, own_edge, recv_edge, mats, house, nt):
    nw = 2 * nt
    count = len(recv)
    cols = 2 * count * LANE
    hbm = pl.BlockSpec(memory_space=pl.ANY)
    shape = jax.ShapeDtypeStruct((nt * WIN, cols), F32)
    return pl.pallas_call(
        functools.partial(sweep_kernel, nt, first, count),
        out_shape=(shape, shape, jax.ShapeDtypeStruct((house, cols), F32)),
        grid_spec=pltpu.PrefetchScalarGridSpec(
            num_scalar_prefetch=1,
            grid=(1,),
            in_specs=[hbm] * (4 + count),
            out_specs=[hbm, hbm, pl.BlockSpec((house, cols), lambda i, place: (0, 0))],
            scratch_shapes=[
                pltpu.VMEM((nw * WIN, cols), F32),
                pltpu.VMEM((nw, 6, WIN, WIN), BF16),
                pltpu.SemaphoreType.DMA((nw, 1 + count)),
                pltpu.SemaphoreType.DMA((nw,)),
                pltpu.SemaphoreType.DMA((nw,)),
            ],
        ),
        compiler_params=params("arbitrary"),
        cost_estimate=cost(nw * 9 * 2 * WIN**2 * cols, nw * WIN * (8 * cols + 6 * WIN)),
    )(place, data, own_edge, recv_edge, mats, *recv)


def update_kernel(first, slab, steps, aliased, place, *refs):
    refs = refs[1:] if aliased else refs
    factor, proj, proj_mate, panel, keep, mate, out, wh, wl, result, sems = refs
    i = pl.program_id(0)
    rows, cols = keep.shape
    width = cols // 2
    me = place[1]

    @pl.when(i == 0)
    def _():
        r = lax.broadcasted_iota(jnp.int32, factor.shape, 0)
        c = lax.broadcasted_iota(jnp.int32, factor.shape, 1)
        uh, ul = split(jnp.where(r <= c, factor[...], 0.0))
        for at, source in enumerate((proj, proj_mate)):
            h, l = split(product(uh, ul, source[...]))
            wh[:, at * cols : (at + 1) * cols] = h
            wl[:, at * cols : (at + 1) * cols] = l

    def copies(step, slot):
        found = []
        for at in range(2):
            core = me if at == 0 else 1 - me
            for x in range(2):
                column = pl.multiple_of((2 * x + core) * slab + first * LANE, LANE)
                start = at * cols + x * width
                found.append(
                    pltpu.make_async_copy(
                        result.at[slot, :, start : start + width],
                        out.at[pl.ds(pl.multiple_of(step * rows, rows), rows), pl.ds(column, width)],
                        sems.at[slot, 2 * at + x],
                    )
                )
        return found

    slot = lax.rem(i, 2)

    @pl.when(i >= 2)
    def _():
        for copy in copies(i - 2, slot):
            copy.wait()

    ph, pl_ = split(panel[...])
    left = jnp.concatenate([ph, ph, pl_], axis=1)
    for at, source in enumerate((keep, mate)):
        span = slice(at * cols, (at + 1) * cols)
        right = jnp.concatenate([wh[:, span], wl[:, span], wh[:, span]], axis=0)
        result[slot, :, span] = source[...] - dot(left, right)
    for copy in copies(i, slot):
        copy.start()

    @pl.when(i == steps - 1)
    def _():
        if steps > 1:
            for copy in copies(i - 1, 1 - slot):
                copy.wait()
        for copy in copies(i, slot):
            copy.wait()


def update_chunk(place, first, out, factor, proj, proj_mate, panel, keep, mate, slab):
    rows, width = panel.shape
    cols = keep.shape[1]
    block = WIN
    aliased = out is not None
    whole = pl.BlockSpec((width, width), lambda i, place: (0, 0))
    weight = pl.BlockSpec((width, cols), lambda i, place: (0, 0))
    data = pl.BlockSpec((block, cols), lambda i, place: (i, 0))
    in_specs = [whole, weight, weight, pl.BlockSpec((block, width), lambda i, place: (i, 0)), data, data]
    args = [factor, proj, proj_mate, panel, keep, mate]
    if aliased:
        in_specs = [pl.BlockSpec(memory_space=pl.ANY)] + in_specs
        args = [out] + args
    return pl.pallas_call(
        functools.partial(update_kernel, first, slab, rows // block, aliased),
        out_shape=jax.ShapeDtypeStruct((rows, 4 * slab), F32),
        grid_spec=pltpu.PrefetchScalarGridSpec(
            num_scalar_prefetch=1,
            grid=(rows // block,),
            in_specs=in_specs,
            out_specs=pl.BlockSpec(memory_space=pl.ANY),
            scratch_shapes=[
                pltpu.VMEM((width, 2 * cols), BF16),
                pltpu.VMEM((width, 2 * cols), BF16),
                pltpu.VMEM((2, block, 2 * cols), F32),
                pltpu.SemaphoreType.DMA((2, 4)),
            ],
        ),
        input_output_aliases={1: 0} if aliased else {},
        compiler_params=params("arbitrary"),
        cost_estimate=cost(6 * rows * width * 2 * cols, 4 * rows * 2 * cols * 2),
    )(place, *args)


def on_device(rows_n, cols_n, eigvecs, v1, v2, f1, f2, panel, panel_factor):
    layer = lax.axis_index("layer")
    row = lax.axis_index("row")
    z = lax.axis_index("col")
    x, core = layer // 2, layer % 2
    place = jnp.stack([x, core, z]).astype(jnp.int32)
    across = [(0, 2), (2, 0), (1, 3), (3, 1)]
    mates = [(0, 1), (1, 0), (2, 3), (3, 2)]
    height, slab = eigvecs.shape
    chip = height // 2
    nt = chip // WIN // 2
    chunks = slab // LANE
    house = panel.shape[1]

    def shifted(value):
        moves = [[(i, (i + s) % cols_n) for i in range(cols_n)] for s in range(1, cols_n)]
        return [value] + [lax.ppermute(value, "col", pairs) for pairs in moves]

    t1, t2, g1, g2 = v1.T, v2.T, f1.T, f2.T
    blank = jnp.zeros((t1.shape[0], HALF), F32)
    top = jnp.concatenate([t1[:, :WIN], t2[:, :HALF], g1[:, :HALF], g2[:, :HALF]], axis=1)
    bottom = jnp.concatenate([t1[:, -WIN:], t2[:, -HALF:], g1[:, -HALF:], blank], axis=1)
    mine = jnp.where(core == 0, top, bottom)
    peer = lax.ppermute(mine, "layer", across)

    source = eigvecs
    sends = []
    for j in range(chunks):
        start = (1 - x) * chip + WIN
        piece = lax.dynamic_slice(source, (start, j * LANE), (chip - 2 * WIN, LANE))
        if j < 2:
            source, piece = lax.optimization_barrier((source, piece))
        sends.append(piece)
    received = [lax.ppermute(sends[j], "layer", across) for j in range(chunks - 1)]

    stacked = jnp.concatenate([t1, t2, g1, g2], axis=1)
    own = shifted(stacked)

    inner_end, outer_end = jnp.where(x == core, mine, peer), jnp.where(x == core, peer, mine)
    pairs = []
    for r in range(rows_n - 1):
        for l in range(4):
            low, high = r * 4 + l, (r + 1) * 4 + l
            pairs.append((high, low) if l % 2 == 0 else (low, high))
    beyond = lax.ppermute(inner_end, ("row", "layer"), pairs)
    edges = jnp.concatenate(
        [
            jnp.where(core == 0, inner_end, beyond),
            outer_end,
            jnp.where(core == 0, beyond, inner_end),
        ],
        axis=1,
    )
    halo_above = lax.ppermute(eigvecs[-WIN:], "row", [(r, r + 1) for r in range(rows_n - 1)])
    halo_below = lax.ppermute(eigvecs[:WIN], "row", [(r + 1, r) for r in range(rows_n - 1)])
    panel_mate = lax.ppermute(panel, "layer", mates)
    own_edges = shifted(edges)
    mate = [lax.ppermute(value, "layer", mates) for value in own]
    mate_edges = [lax.ppermute(value, "layer", mates) for value in own_edges]

    bh, bl = edge_matrices(place, own_edges, mate_edges)
    above = jnp.stack([halo_above, eigvecs[chip - WIN : chip], eigvecs[-WIN:]])
    below = jnp.stack([eigvecs[:WIN], eigvecs[chip : chip + WIN], halo_below])
    swept = sweep_edges(bh, bl, above, below)
    edge_send = jnp.stack(
        [
            lax.dynamic_index_in_dim(swept[:, 1], 1 - x, 0, keepdims=False),
            lax.dynamic_index_in_dim(swept[:, 0], 2 - x, 0, keepdims=False),
        ]
    )
    edge_recv = lax.ppermute(edge_send, "layer", across)
    mats = window_matrices(place, own, mate, panel, panel_mate, nt)
    received.append(lax.ppermute(sends[-1], "layer", across))

    def swept_chunk(first, count):
        return sweep_chunk(
            place, first, eigvecs, received[first : first + count], swept, edge_recv, mats, house, nt,
        )

    ring = [(r, (r + 1) % rows_n) for r in range(rows_n)]

    def summed(partial, halves):
        if halves and rows_n == 2:
            half = partial.shape[1] // 2
            away = lax.dynamic_slice(partial, (0, (1 - row) * half), (house, half))
            home = lax.dynamic_slice(partial, (0, row * half), (house, half))
            home = home + lax.ppermute(away, "row", ring)
            home = home + lax.ppermute(home, "layer", across)
            away = lax.ppermute(home, "row", ring)
            first = row == 0
            return jnp.concatenate(
                [jnp.where(first, home, away), jnp.where(first, away, home)], axis=1
            )
        total = partial + lax.ppermute(partial, "layer", across)
        moving = total
        for _ in range(rows_n - 1):
            moving = lax.ppermute(moving, "row", ring)
            total = total + moving
        return total

    def updated(first, out, keep, other, total):
        total_mate = lax.ppermute(total, "layer", mates)
        return update_chunk(
            place, first, out, panel_factor, total, total_mate, panel, keep, other, slab,
        )

    lead = chunks - 1
    keep_a, send_a, part_a = swept_chunk(0, lead)
    other_a = lax.ppermute(send_a, "layer", mates)
    keep_b, send_b, part_b = swept_chunk(lead, 1)
    other_b = lax.ppermute(send_b, "layer", mates)
    total_a = summed(part_a, True)
    total_b = summed(part_b, False)
    out = updated(0, None, keep_a, other_a, total_a)
    return updated(lead, out, keep_b, other_b, total_b)


def solution(mesh):
    in_specs = (
        P("row", ("col", "layer")),
        P(("row", "layer"), "col"),
        P(("row", "layer"), "col"),
        P(("row", "layer"), "col"),
        P(("row", "layer"), "col"),
        P(("row", "layer"), None),
        P(),
    )

    def body(*args):
        return on_device(mesh.shape["row"], mesh.shape["col"], *args)

    return jax.shard_map(
        body,
        mesh=mesh,
        in_specs=in_specs,
        out_specs=P(("row", "layer"), "col"),
        check_vma=False,
    )
```

profile of v0, /device:TPU:0, one launch (start us, length us, event | category | flops | bytes accessed | tf_op | source)
XLA Modules:
  0.0 390.8 jit_solution(16895606545873947990)
XLA Ops:
  0.0 0.7 slice.57
  0.7 0.8 fusion.1
  1.5 0.8 fusion.2
  2.3 3.0 collective-permute-start
  5.3 2.4 collective-permute-done
  7.8 1.3 collective-permute-start.1
  9.1 1.2 pad_maximum_fusion.3.refs_0_
  10.3 4.2 %collective-permute-start.14 = (f32[32,6144]{1,0:T(8,128)S(1)}, f32[32,6144]{1,0:T(8,128)}, u32[]{:S(2)}, u32[]{:S(2)}) collective-permute-start(f32[32,6144]{1,0:T(8,128)S(1)} %pad_maximum_fusion.3.refs_0_), channel_id=1, source_target_pairs={{0,12},{4,0},{8,4},{12,8},{1,13},{5,1},{9,5},{13,9},{2,14},{6,2},{... | collective-permute-start | bytes 2359304 | tf_op jit(solution)/shard_map/ppermute | solution.py:462
  14.6 0.3 collective-permute-start.5
  14.9 3.5 collective-permute-start.4
  18.4 2.8 slice_bitcast_fusion.2
  21.2 1.3 collective-permute-start.10
  22.5 32.1 %collective-permute-done.4.refs_3_ = f32[32,1920]{1,0:T(8,128)S(1)} collective-permute-done((f32[32,1920]{1,0:T(8,128)S(1)}, f32[32,1920]{1,0:T(8,128)S(1)}, u32[]{:S(2)}, u32[]{:S(2)}) %collective-permute-start.4) | collective-permute-done | bytes 245792 | tf_op jit(solution)/shard_map/ppermute | solution.py:462
  54.6 3.8 collective-permute-start.9
  58.4 23.1 %collective-permute-done.3.refs_2_ = f32[32,1920]{1,0:T(8,128)} collective-permute-done((f32[32,1920]{1,0:T(8,128)S(1)}, f32[32,1920]{1,0:T(8,128)}, u32[]{:S(2)}, u32[]{:S(2)}) %collective-permute-start.3) | collective-permute-done | bytes 245792 | tf_op jit(solution)/shard_map/ppermute | solution.py:462
  81.5 0.9 collective-permute-start.2
  82.4 2.9 constant_dynamic-slice_fusion.1
  85.3 5.5 %collective-permute-done.2.refs_1_ = f32[32,1920]{1,0:T(8,128)S(1)} collective-permute-done((f32[32,1920]{1,0:T(8,128)S(1)}, f32[32,1920]{1,0:T(8,128)S(1)}, u32[]{:S(2)}, u32[]{:S(2)}) %collective-permute-start.2) | collective-permute-done | bytes 245792 | tf_op jit(solution)/shard_map/ppermute | solution.py:462
  90.9 3.0 constant_dynamic-slice_fusion.2
  93.9 0.5 collective-permute-start.15
  94.4 0.2 collective-permute-start.7
  94.6 0.4 collective-permute-start.18
  95.0 0.1 copy-done.9
  95.2 0.1 copy-done.18
  95.3 0.1 collective-permute-start.17
  95.4 4.2 %constant_dynamic-slice_fusion.3 = (f32[3584,128]{1,0:T(8,128)}, f32[3584,128]{1,0:T(8,128)}) fusion(f32[8192,512]{1,0:T(8,128)} %refs_0_.5, s32[]{:T(128)S(6)} %select_n.80), kind=kLoop, calls=%fused_computation.22 | loop fusion | bytes 7340036 | tf_op jit(solution)/shard_map/dynamic_slice | solution.py:475
  99.6 0.5 collective-permute-start.6
  100.0 0.7 pad_add_fusion.place
  100.7 2.7 pad_maximum_fusion.1.below
  103.4 0.3 collective-permute-start.19
  103.7 0.4 copy-done.19
  104.1 1.3 pad_maximum_fusion.above
  105.3 6.6 %edge_matrices.1 = (bf16[3,3,256,256]{3,2,1,0:T(8,128)(2,1)}, bf16[3,3,256,256]{3,2,1,0:T(8,128)(2,1)}) custom-call(s32[3]{0:T(128)} %pad_add_fusion.place, f32[32,1920]{1,0:T(8,128)} %copy-done.14, f32[32,1920]{1,0:T(8,128)} %copy-done.17, f32[32,1920]{1,0:T(8,128)} %collective-permute-done.3.refs_2_, f32[32,1920]{1,0:T(8,128)} %copy-done.16, ...), custom_call_target="tpu_custom_call" | custom-call | flops 2000000000 | bytes 4194304 | tf_op jit(solution)/shard_map/edge_matrices/pallas_call | solution.py:87
  112.0 1.5 collective-permute-start.21
  113.5 2.4 collective-permute-done.12.refs_1_
  115.9 1.5 collective-permute-start.20
  117.4 0.5 collective-permute-start.22
  117.9 8.2 %sweep_edges.1.refs_1_ = f32[3,2,256,512]{3,2,1,0:T(8,128)} custom-call(bf16[3,3,256,256]{3,2,1,0:T(8,128)(2,1)} %get-tuple-element.17.high, bf16[3,3,256,256]{3,2,1,0:T(8,128)(2,1)} %get-tuple-element.18.low, f32[3,256,512]{2,1,0:T(8,128)} %pad_maximum_fusion.above, f32[3,256,512]{2,1,0:T(8,128)} %pad_maximum_fusion.1.below), custom_call_target="tpu_custom_call" | custom-call | flops 6000000000 | bytes 8388608 | tf_op jit(solution)/shard_map/sweep_edges/pallas_call | solution.py:179
  126.1 2.2 fusion
  128.4 1.1 pad_maximum_fusion.2
  129.5 1.5 collective-permute-start.11
  131.0 16.5 %window_matrices.1.refs_3_ = bf16[16,6,256,256]{3,2,1,0:T(8,128)(2,1)} custom-call(s32[3]{0:T(128)} %pad_add_fusion.place, f32[32,6144]{1,0:T(8,128)} %copy-done.1, f32[32,6144]{1,0:T(8,128)} %collective-permute-done.12.refs_1_, f32[32,6144]{1,0:T(8,128)} %collective-permute-done.13.refs_2_, f32[32,6144]{1,0:T(8,128)} %collective-permute-done.14.refs_3_, ...), custom_call_target="tpu_custom_call" | custom-call | flops 6000000000 | bytes 25165824 | tf_op jit(solution)/shard_map/window_matrices/pallas_call | solution.py:145
  147.5 108.1 %collective-permute-done.11.refs_2_ = f32[2,256,512]{2,1,0:T(8,128)} collective-permute-done((f32[2,256,512]{2,1,0:T(8,128)}, f32[2,256,512]{2,1,0:T(8,128)}, u32[]{:S(2)}, u32[]{:S(2)}) %collective-permute-start.11) | collective-permute-done | bytes 1048608 | tf_op jit(solution)/shard_map/ppermute | solution.py:516
  255.6 23.1 %shard_map.73 = (f32[2048,768]{1,0:T(8,128)}, f32[2048,768]{1,0:T(8,128)}, f32[256,768]{1,0:T(8,128)}) custom-call(s32[3]{0:T(128)} %pad_add_fusion.place, f32[8192,512]{1,0:T(8,128)} %refs_0_.5, f32[3,2,256,512]{3,2,1,0:T(8,128)} %sweep_edges.1.refs_1_, f32[2,256,512]{2,1,0:T(8,128)} %collective-permute-done.11.refs_2_, ...), custom_call_target="tpu_custom_call" | custom-call | flops 14495514624 | bytes 31457280 | tf_op jit(solution)/shard_map/pallas_call | solution.py:332
  278.7 0.1 collective-permute-start.27
  278.8 1.5 collective-permute-start.28
  280.4 1.0 constant_dynamic-slice_fusion
  281.5 11.1 %collective-permute-done.23 = f32[256,384]{1,0:T(8,128)S(1)} collective-permute-done((f32[256,384]{1,0:T(8,128)S(1)}, f32[256,384]{1,0:T(8,128)S(1)}, u32[]{:S(2)}, u32[]{:S(2)}) %collective-permute-start.23) | collective-permute-done | bytes 393248 | tf_op jit(solution)/shard_map/ppermute | solution.py:532
  292.6 1.0 dynamic-slice_add_fusion
  293.6 0.6 collective-permute-start.24
  294.3 27.6 %collective-permute-done.28.refs_4_ = f32[3584,128]{1,0:T(8,128)} collective-permute-done((f32[3584,128]{1,0:T(8,128)S(1)}, f32[3584,128]{1,0:T(8,128)}, u32[]{:S(2)}, u32[]{:S(2)}) %collective-permute-start.28) | collective-permute-done | bytes 1835040 | tf_op jit(solution)/shard_map/ppermute | solution.py:518
  321.9 11.7 %shard_map.75 = (f32[2048,256]{1,0:T(8,128)}, f32[2048,256]{1,0:T(8,128)}, f32[256,256]{1,0:T(8,128)}) custom-call(s32[3]{0:T(128)} %pad_add_fusion.place, f32[8192,512]{1,0:T(8,128)} %refs_0_.5, f32[3,2,256,512]{3,2,1,0:T(8,128)} %sweep_edges.1.refs_1_, f32[2,256,512]{2,1,0:T(8,128)} %collective-permute-done.11.refs_2_, ...), custom_call_target="tpu_custom_call" | custom-call | flops 4831838208 | bytes 14680064 | tf_op jit(solution)/shard_map/pallas_call | solution.py:332
  333.8 11.5 %collective-permute-done.25 = f32[256,384]{1,0:T(8,128)S(1)} collective-permute-done((f32[256,384]{1,0:T(8,128)S(1)}, f32[256,384]{1,0:T(8,128)S(1)}, u32[]{:S(2)}, u32[]{:S(2)}) %collective-permute-start.25) | collective-permute-done | bytes 393248 | tf_op jit(solution)/shard_map/ppermute | solution.py:534
  345.4 0.1 collective-permute-start.26
  345.5 1.5 collective-permute-start.29
  347.1 7.2 %collective-permute-done.29 = f32[256,256]{1,0:T(8,128)S(1)} collective-permute-done((f32[256,256]{1,0:T(8,128)S(1)}, f32[256,256]{1,0:T(8,128)S(1)}, u32[]{:S(2)}, u32[]{:S(2)}) %collective-permute-start.29) | collective-permute-done | bytes 262176 | tf_op jit(solution)/shard_map/ppermute | solution.py:539
  354.2 0.4 collective-permute-start.30
  354.6 7.5 %collective-permute-done.30 = f32[256,256]{1,0:T(8,128)S(1)} collective-permute-done((f32[256,256]{1,0:T(8,128)S(1)}, f32[256,256]{1,0:T(8,128)S(1)}, u32[]{:S(2)}, u32[]{:S(2)}) %collective-permute-start.30) | collective-permute-done | bytes 262176 | tf_op jit(solution)/shard_map/ppermute | solution.py:542
  362.1 0.1 collective-permute-start.31
  362.2 0.9 copy-done.8
  363.1 16.7 %shard_map.74.refs_0_ = f32[2048,2048]{1,0:T(8,128)} custom-call(s32[3]{0:T(128)} %pad_add_fusion.place, f32[256,256]{1,0:T(8,128)} %refs_1_.1, f32[256,768]{1,0:T(8,128)} %copy-done.2, f32[256,768]{1,0:T(8,128)} %copy-done.8, f32[2048,256]{1,0:T(8,128)} %refs_4_.1, f32[2048,768]{1,0:T(8,128)} %get-tuple-element.24.refs_4_, ...), custom_call_target="tpu_custom_call" | custom-call | flops 4831838208 | bytes 25165824 | tf_op jit(solution)/shard_map/pallas_call | solution.py:425
  379.8 0.7 copy-done.12
  380.5 0.7 copy-done.4
  381.2 9.4 %shard_map.76 = f32[2048,2048]{1,0:T(8,128)} custom-call(s32[3]{0:T(128)} %pad_add_fusion.place, f32[2048,2048]{1,0:T(8,128)} %shard_map.74.refs_0_, f32[256,256]{1,0:T(8,128)} %refs_1_.1, f32[256,256]{1,0:T(8,128)} %copy-done.6, f32[256,256]{1,0:T(8,128)} %copy-done.12, f32[2048,256]{1,0:T(8,128)} %refs_4_.1, ...), custom_call_target="tpu_custom_call", output_to_operand_aliasing={{}: (1, {})} | custom-call | flops 1610612736 | bytes 8388608 | tf_op jit(solution)/shard_map/pallas_call | solution.py:425
  (77 shorter events, 0.8 us)
Async XLA Ops:
  2.3 5.5 %collective-permute-start = (f32[32,640]{1,0:T(8,128)S(1)}, f32[32,640]{1,0:T(8,128)S(1)}, u32[]{:S(2)}, u32[]{:S(2)}) collective-permute-start(f32[32,640]{1,0:T(8,128)S(1)} %maximum_select_fusion), channel_id=1, source_target_pairs={{0,2},{2,0},{1,3},{3,1},{4,6},{6,4},{5,7},{7,5},{8,10},{10,8},{9,1... | collective-permute-start | bytes 245768 | tf_op jit(solution)/shard_map/ppermute | solution.py:469
  7.8 6.7 %collective-permute-start.1 = (f32[32,640]{1,0:T(8,128)S(1)}, f32[32,640]{1,0:T(8,128)S(1)}, u32[]{:S(2)}, u32[]{:S(2)}) collective-permute-start(f32[32,640]{1,0:T(8,128)S(1)} %get-tuple-element.48), channel_id=1, source_target_pairs={{16,0},{1,17},{18,2},{3,19},{20,4},{5,21},{22,6},{7,23},{24,8},{9,... | collective-permute-start | bytes 245768 | tf_op jit(solution)/shard_map/ppermute | solution.py:490
  10.3 84.0 %copy-start.1 = (f32[32,6144]{1,0:T(8,128)}, f32[32,6144]{1,0:T(8,128)S(1)}, u32[]{:S(2)}) copy-start(f32[32,6144]{1,0:T(8,128)S(1)} %pad_maximum_fusion.3.refs_0_) | copy-start | bytes 2359300
  10.3 84.3 %collective-permute-start.14 = (f32[32,6144]{1,0:T(8,128)S(1)}, f32[32,6144]{1,0:T(8,128)}, u32[]{:S(2)}, u32[]{:S(2)}) collective-permute-start(f32[32,6144]{1,0:T(8,128)S(1)} %pad_maximum_fusion.3.refs_0_), channel_id=1, source_target_pairs={{0,12},{4,0},{8,4},{12,8},{1,13},{5,1},{9,5},{13,9},{2,14},{6,2},{... | collective-permute-start | bytes 2359304 | tf_op jit(solution)/shard_map/ppermute | solution.py:462
  14.5 80.5 %collective-permute-start.13 = (f32[32,6144]{1,0:T(8,128)S(1)}, f32[32,6144]{1,0:T(8,128)}, u32[]{:S(2)}, u32[]{:S(2)}) collective-permute-start(f32[32,6144]{1,0:T(8,128)S(1)} %pad_maximum_fusion.3.refs_0_), channel_id=1, source_target_pairs={{0,8},{4,12},{8,0},{12,4},{1,9},{5,13},{9,1},{13,5},{2,10},{6,14},... | collective-permute-start | bytes 2359304 | tf_op jit(solution)/shard_map/ppermute | solution.py:462
  14.6 67.0 %copy-start.14 = (f32[32,1920]{1,0:T(8,128)}, f32[32,1920]{1,0:T(8,128)S(1)}, u32[]{:S(2)}) copy-start(f32[32,1920]{1,0:T(8,128)S(1)} %pad_maximum_fusion.5.refs_0_) | copy-start | bytes 737284
  14.6 6.7 %collective-permute-start.5 = (f32[32,1920]{1,0:T(8,128)S(1)}, f32[32,1920]{1,0:T(8,128)S(1)}, u32[]{:S(2)}, u32[]{:S(2)}) collective-permute-start(f32[32,1920]{1,0:T(8,128)S(1)} %pad_maximum_fusion.5.refs_0_), channel_id=1, source_target_pairs={{0,1},{1,0},{2,3},{3,2},{4,5},{5,4},{6,7},{7,6},{8,9},{9,8},{10,11... | collective-permute-start | bytes 737288 | tf_op jit(solution)/shard_map/ppermute | solution.py:504
  14.9 39.7 %collective-permute-start.4 = (f32[32,1920]{1,0:T(8,128)S(1)}, f32[32,1920]{1,0:T(8,128)S(1)}, u32[]{:S(2)}, u32[]{:S(2)}) collective-permute-start(f32[32,1920]{1,0:T(8,128)S(1)} %pad_maximum_fusion.5.refs_0_), channel_id=1, source_target_pairs={{0,12},{4,0},{8,4},{12,8},{1,13},{5,1},{9,5},{13,9},{2,14},{6,2},{... | collective-permute-start | bytes 737288 | tf_op jit(solution)/shard_map/ppermute | solution.py:462
  18.4 63.1 %collective-permute-start.3 = (f32[32,1920]{1,0:T(8,128)S(1)}, f32[32,1920]{1,0:T(8,128)}, u32[]{:S(2)}, u32[]{:S(2)}) collective-permute-start(f32[32,1920]{1,0:T(8,128)S(1)} %pad_maximum_fusion.5.refs_0_), channel_id=1, source_target_pairs={{0,8},{4,12},{8,0},{12,4},{1,9},{5,13},{9,1},{13,5},{2,10},{6,14},... | collective-permute-start | bytes 737288 | tf_op jit(solution)/shard_map/ppermute | solution.py:462
  21.2 64.1 %copy-start.15 = (f32[32,1920]{1,0:T(8,128)}, f32[32,1920]{1,0:T(8,128)S(1)}, u32[]{:S(2)}) copy-start(f32[32,1920]{1,0:T(8,128)S(1)} %collective-permute-done.5.refs_4_) | copy-start | bytes 737284
  21.2 72.6 %collective-permute-start.10 = (f32[256,512]{1,0:T(8,128)S(1)}, f32[256,512]{1,0:T(8,128)S(1)}, u32[]{:S(2)}, u32[]{:S(2)}) collective-permute-start(f32[256,512]{1,0:T(8,128)S(1)} %get-tuple-element.34), channel_id=1, source_target_pairs={{16,0},{17,1},{18,2},{19,3},{20,4},{21,5},{22,6},{23,7},{24,8},{25... | collective-permute-start | bytes 1572872 | tf_op jit(solution)/shard_map/ppermute | solution.py:500
  54.6 36.3 %copy-start.16 = (f32[32,1920]{1,0:T(8,128)}, f32[32,1920]{1,0:T(8,128)S(1)}, u32[]{:S(2)}) copy-start(f32[32,1920]{1,0:T(8,128)S(1)} %collective-permute-done.4.refs_3_) | copy-start | bytes 737284
  54.6 39.8 %collective-permute-start.9 = (f32[256,512]{1,0:T(8,128)S(1)}, f32[256,512]{1,0:T(8,128)S(1)}, u32[]{:S(2)}, u32[]{:S(2)}) collective-permute-start(f32[256,512]{1,0:T(8,128)S(1)} %get-tuple-element.36), channel_id=1, source_target_pairs={{0,16},{1,17},{2,18},{3,19},{4,20},{5,21},{6,22},{7,23},{8,24},{9,... | collective-permute-start | bytes 1572872 | tf_op jit(solution)/shard_map/ppermute | solution.py:499
  81.5 9.3 %collective-permute-start.2 = (f32[32,1920]{1,0:T(8,128)S(1)}, f32[32,1920]{1,0:T(8,128)S(1)}, u32[]{:S(2)}, u32[]{:S(2)}) collective-permute-start(f32[32,1920]{1,0:T(8,128)S(1)} %pad_maximum_fusion.5.refs_0_), channel_id=1, source_target_pairs={{0,4},{4,8},{8,12},{12,0},{1,5},{5,9},{9,13},{13,1},{2,6},{6,10},{... | collective-permute-start | bytes 737288 | tf_op jit(solution)/shard_map/ppermute | solution.py:462
  90.9 3.0 copy-start.17
  90.9 3.6 collective-permute-start.8
  93.9 1.2 copy-start.11
  93.9 18.1 %collective-permute-start.15 = (f32[32,6144]{1,0:T(8,128)S(1)}, f32[32,6144]{1,0:T(8,128)}, u32[]{:S(2)}, u32[]{:S(2)}) collective-permute-start(f32[32,6144]{1,0:T(8,128)S(1)} %pad_maximum_fusion.3.refs_0_), channel_id=1, source_target_pairs={{0,1},{1,0},{2,3},{3,2},{4,5},{5,4},{6,7},{7,6},{8,9},{9,8},{10,11... | collective-permute-start | bytes 2359304 | tf_op jit(solution)/shard_map/ppermute | solution.py:503
  94.4 0.8 copy-start.9
  94.4 21.5 %collective-permute-start.12 = (f32[32,6144]{1,0:T(8,128)S(1)}, f32[32,6144]{1,0:T(8,128)}, u32[]{:S(2)}, u32[]{:S(2)}) collective-permute-start(f32[32,6144]{1,0:T(8,128)S(1)} %pad_maximum_fusion.3.refs_0_), channel_id=1, source_target_pairs={{0,4},{4,8},{8,12},{12,0},{1,5},{5,9},{9,13},{13,1},{2,6},{6,10},{... | collective-permute-start | bytes 2359304 | tf_op jit(solution)/shard_map/ppermute | solution.py:462
  94.4 0.8 copy-start.18
  94.4 5.1 %collective-permute-start.7 = (f32[32,1920]{1,0:T(8,128)}, f32[32,1920]{1,0:T(8,128)}, u32[]{:S(2)}, u32[]{:S(2)}) collective-permute-start(f32[32,1920]{1,0:T(8,128)} %collective-permute-done.3.refs_2_), channel_id=1, source_target_pairs={{0,1},{1,0},{2,3},{3,2},{4,5},{5,4},{6,7},{7,6},{8,9},{9,8},{10,11... | collective-permute-start | bytes 737288 | tf_op jit(solution)/shard_map/ppermute | solution.py:504
  94.6 22.7 %collective-permute-start.18 = (f32[32,6144]{1,0:T(8,128)}, f32[32,6144]{1,0:T(8,128)}, u32[]{:S(2)}, u32[]{:S(2)}) collective-permute-start(f32[32,6144]{1,0:T(8,128)} %collective-permute-done.14.refs_3_), channel_id=1, source_target_pairs={{0,1},{1,0},{2,3},{3,2},{4,5},{5,4},{6,7},{7,6},{8,9},{9,8},{10,11... | collective-permute-start | bytes 2359304 | tf_op jit(solution)/shard_map/ppermute | solution.py:503
  95.3 22.6 %collective-permute-start.17 = (f32[32,6144]{1,0:T(8,128)}, f32[32,6144]{1,0:T(8,128)}, u32[]{:S(2)}, u32[]{:S(2)}) collective-permute-start(f32[32,6144]{1,0:T(8,128)} %collective-permute-done.13.refs_2_), channel_id=1, source_target_pairs={{0,1},{1,0},{2,3},{3,2},{4,5},{5,4},{6,7},{7,6},{8,9},{9,8},{10,11... | collective-permute-start | bytes 2359304 | tf_op jit(solution)/shard_map/ppermute | solution.py:503
  99.5 3.8 copy-start
  99.5 4.5 %copy-start.3 = (f32[1,256,512]{2,1,0:T(8,128)S(1)}, f32[1,256,512]{2,1,0:T(8,128)}, u32[]{:S(2)}) copy-start(f32[1,256,512]{2,1,0:T(8,128)} %get-tuple-element.35) | copy-start | bytes 1572868
  99.5 4.5 %copy-start.10 = (f32[256,512]{1,0:T(8,128)S(1)}, f32[256,512]{1,0:T(8,128)}, u32[]{:S(2)}) copy-start(f32[256,512]{1,0:T(8,128)} %copy-done.9) | copy-start | bytes 1572868
  99.6 3.8 collective-permute-start.6
  103.4 0.7 copy-start.19
  103.4 27.6 %collective-permute-start.19 = (f32[2048,256]{1,0:T(8,128)S(1)}, f32[2048,256]{1,0:T(8,128)}, u32[]{:S(2)}, u32[]{:S(2)}) collective-permute-start(f32[2048,256]{1,0:T(8,128)S(1)} %copy-done), channel_id=1, source_target_pairs={{0,1},{1,0},{2,3},{3,2},{4,5},{5,4},{6,7},{7,6},{8,9},{9,8},{10,11... | collective-permute-start | bytes 6291464 | tf_op jit(solution)/shard_map/ppermute | solution.py:501
  112.0 143.6 %collective-permute-start.21 = (f32[3584,128]{1,0:T(8,128)}, f32[3584,128]{1,0:T(8,128)}, u32[]{:S(2)}, u32[]{:S(2)}) collective-permute-start(f32[3584,128]{1,0:T(8,128)} %constant_dynamic-slice_fusion.2), channel_id=1, source_target_pairs={{0,2},{2,0},{1,3},{3,1},{4,6},{6,4},{5,7},{7,5},{8,10},{10,8},{9,1... | collective-permute-start | bytes 5505032 | tf_op jit(solution)/shard_map/ppermute | solution.py:479
  115.9 139.7 %collective-permute-start.20 = (f32[3584,128]{1,0:T(8,128)}, f32[3584,128]{1,0:T(8,128)}, u32[]{:S(2)}, u32[]{:S(2)}) collective-permute-start(f32[3584,128]{1,0:T(8,128)} %constant_dynamic-slice_fusion.1), channel_id=1, source_target_pairs={{0,2},{2,0},{1,3},{3,1},{4,6},{6,4},{5,7},{7,5},{8,10},{10,8},{9,1... | collective-permute-start | bytes 5505032 | tf_op jit(solution)/shard_map/ppermute | solution.py:479
  117.4 138.2 %collective-permute-start.22 = (f32[3584,128]{1,0:T(8,128)}, f32[3584,128]{1,0:T(8,128)}, u32[]{:S(2)}, u32[]{:S(2)}) collective-permute-start(f32[3584,128]{1,0:T(8,128)} %get-tuple-element.30), channel_id=1, source_target_pairs={{0,2},{2,0},{1,3},{3,1},{4,6},{6,4},{5,7},{7,5},{8,10},{10,8},{9,1... | collective-permute-start | bytes 5505032 | tf_op jit(solution)/shard_map/ppermute | solution.py:479
  117.9 11.6 %collective-permute-start.16 = (f32[32,6144]{1,0:T(8,128)}, f32[32,6144]{1,0:T(8,128)S(1)}, u32[]{:S(2)}, u32[]{:S(2)}) collective-permute-start(f32[32,6144]{1,0:T(8,128)} %collective-permute-done.12.refs_1_), channel_id=1, source_target_pairs={{0,1},{1,0},{2,3},{3,2},{4,5},{5,4},{6,7},{7,6},{8,9},{9,8},{10,11... | collective-permute-start | bytes 2359304 | tf_op jit(solution)/shard_map/ppermute | solution.py:503
  129.5 1.5 copy-start.7
  129.5 126.1 %collective-permute-start.11 = (f32[2,256,512]{2,1,0:T(8,128)}, f32[2,256,512]{2,1,0:T(8,128)}, u32[]{:S(2)}, u32[]{:S(2)}) collective-permute-start(f32[2,256,512]{2,1,0:T(8,128)} %pad_maximum_fusion.2), channel_id=1, source_target_pairs={{0,2},{2,0},{1,3},{3,1},{4,6},{6,4},{5,7},{7,5},{8,10},{10,8},{9,1... | collective-permute-start | bytes 3145736 | tf_op jit(solution)/shard_map/ppermute | solution.py:516
  147.5 131.3 %copy-start.5 = (f32[3584,128]{1,0:T(8,128)S(1)}, f32[3584,128]{1,0:T(8,128)}, u32[]{:S(2)}) copy-start(f32[3584,128]{1,0:T(8,128)} %get-tuple-element.29) | copy-start | bytes 5505028
  278.7 84.4 %collective-permute-start.27 = (f32[2048,768]{1,0:T(8,128)}, f32[2048,768]{1,0:T(8,128)}, u32[]{:S(2)}, u32[]{:S(2)}) collective-permute-start(f32[2048,768]{1,0:T(8,128)} %get-tuple-element.25), channel_id=1, source_target_pairs={{0,1},{1,0},{2,3},{3,2},{4,5},{5,4},{6,7},{7,6},{8,9},{9,8},{10,11... | collective-permute-start | bytes 18874376 | tf_op jit(solution)/shard_map/ppermute | solution.py:554
  278.8 43.1 %collective-permute-start.28 = (f32[3584,128]{1,0:T(8,128)S(1)}, f32[3584,128]{1,0:T(8,128)}, u32[]{:S(2)}, u32[]{:S(2)}) collective-permute-start(f32[3584,128]{1,0:T(8,128)S(1)} %copy-done.5), channel_id=1, source_target_pairs={{0,2},{2,0},{1,3},{3,1},{4,6},{6,4},{5,7},{7,5},{8,10},{10,8},{9,1... | collective-permute-start | bytes 5505032 | tf_op jit(solution)/shard_map/ppermute | solution.py:518
  281.4 11.2 %collective-permute-start.23 = (f32[256,384]{1,0:T(8,128)S(1)}, f32[256,384]{1,0:T(8,128)S(1)}, u32[]{:S(2)}, u32[]{:S(2)}) collective-permute-start(f32[256,384]{1,0:T(8,128)S(1)} %constant_dynamic-slice_fusion), channel_id=1, source_target_pairs={{0,16},{16,0},{1,17},{17,1},{2,18},{18,2},{3,19},{19,3},{4,20},{20... | collective-permute-start | bytes 1179656 | tf_op jit(solution)/shard_map/ppermute | solution.py:532
  293.6 40.0 %collective-permute-start.24 = (f32[256,384]{1,0:T(8,128)S(1)}, f32[256,384]{1,0:T(8,128)S(1)}, u32[]{:S(2)}, u32[]{:S(2)}) collective-permute-start(f32[256,384]{1,0:T(8,128)S(1)} %dynamic-slice_add_fusion), channel_id=1, source_target_pairs={{0,2},{2,0},{1,3},{3,1},{4,6},{6,4},{5,7},{7,5},{8,10},{10,8},{9,1... | collective-permute-start | bytes 1179656 | tf_op jit(solution)/shard_map/ppermute | solution.py:533
  333.6 46.2 %collective-permute-start.32 = (f32[2048,256]{1,0:T(8,128)}, f32[2048,256]{1,0:T(8,128)S(1)}, u32[]{:S(2)}, u32[]{:S(2)}) collective-permute-start(f32[2048,256]{1,0:T(8,128)} %get-tuple-element.28), channel_id=1, source_target_pairs={{0,1},{1,0},{2,3},{3,2},{4,5},{5,4},{6,7},{7,6},{8,9},{9,8},{10,11... | collective-permute-start | bytes 6291464 | tf_op jit(solution)/shard_map/ppermute | solution.py:556
  333.7 11.8 %copy-start.13 = (f32[256,256]{1,0:T(8,128)S(1)}, f32[256,256]{1,0:T(8,128)}, u32[]{:S(2)}) copy-start(f32[256,256]{1,0:T(8,128)} %get-tuple-element.26) | copy-start | bytes 786436
  333.7 11.6 %collective-permute-start.25 = (f32[256,384]{1,0:T(8,128)S(1)}, f32[256,384]{1,0:T(8,128)S(1)}, u32[]{:S(2)}, u32[]{:S(2)}) collective-permute-start(f32[256,384]{1,0:T(8,128)S(1)} %add.54), channel_id=1, source_target_pairs={{0,16},{16,0},{1,17},{17,1},{2,18},{18,2},{3,19},{19,3},{4,20},{20... | collective-permute-start | bytes 1179656 | tf_op jit(solution)/shard_map/ppermute | solution.py:534
  345.4 17.7 %copy-start.2 = (f32[256,768]{1,0:T(8,128)}, f32[256,768]{1,0:T(8,128)S(1)}, u32[]{:S(2)}) copy-start(f32[256,768]{1,0:T(8,128)S(1)} %pad_maximum_fusion.4.refs_1_) | copy-start | bytes 2359300
  345.4 16.8 %collective-permute-start.26 = (f32[256,768]{1,0:T(8,128)S(1)}, f32[256,768]{1,0:T(8,128)S(1)}, u32[]{:S(2)}, u32[]{:S(2)}) collective-permute-start(f32[256,768]{1,0:T(8,128)S(1)} %pad_maximum_fusion.4.refs_1_), channel_id=1, source_target_pairs={{0,1},{1,0},{2,3},{3,2},{4,5},{5,4},{6,7},{7,6},{8,9},{9,8},{10,11... | collective-permute-start | bytes 2359304 | tf_op jit(solution)/shard_map/ppermute | solution.py:547
  345.5 8.7 %collective-permute-start.29 = (f32[256,256]{1,0:T(8,128)S(1)}, f32[256,256]{1,0:T(8,128)S(1)}, u32[]{:S(2)}, u32[]{:S(2)}) collective-permute-start(f32[256,256]{1,0:T(8,128)S(1)} %copy-done.13), channel_id=1, source_target_pairs={{0,2},{2,0},{1,3},{3,1},{4,6},{6,4},{5,7},{7,5},{8,10},{10,8},{9,1... | collective-permute-start | bytes 786440 | tf_op jit(solution)/shard_map/ppermute | solution.py:539
  354.2 7.8 %collective-permute-start.30 = (f32[256,256]{1,0:T(8,128)S(1)}, f32[256,256]{1,0:T(8,128)S(1)}, u32[]{:S(2)}, u32[]{:S(2)}) collective-permute-start(f32[256,256]{1,0:T(8,128)S(1)} %add.55), channel_id=1, source_target_pairs={{0,16},{16,0},{1,17},{17,1},{2,18},{18,2},{3,19},{19,3},{4,20},{20... | collective-permute-start | bytes 786440 | tf_op jit(solution)/shard_map/ppermute | solution.py:542
  362.1 17.6 %copy-start.6 = (f32[256,256]{1,0:T(8,128)}, f32[256,256]{1,0:T(8,128)S(1)}, u32[]{:S(2)}) copy-start(f32[256,256]{1,0:T(8,128)S(1)} %add.56.refs_2_) | copy-start | bytes 786436
  362.1 17.6 %collective-permute-start.31 = (f32[256,256]{1,0:T(8,128)S(1)}, f32[256,256]{1,0:T(8,128)S(1)}, u32[]{:S(2)}, u32[]{:S(2)}) collective-permute-start(f32[256,256]{1,0:T(8,128)S(1)} %add.56.refs_2_), channel_id=1, source_target_pairs={{0,1},{1,0},{2,3},{3,2},{4,5},{5,4},{6,7},{7,6},{8,9},{9,8},{10,11... | collective-permute-start | bytes 786440 | tf_op jit(solution)/shard_map/ppermute | solution.py:547
  362.2 0.9 copy-start.8
  379.8 0.7 copy-start.12
  379.8 1.4 copy-start.4
where the time goes:
time: 392 us; the launch traced here: 391 us
  waiting for transfers between devices  239 us (61%)
  Pallas kernels  92.2 us (24%)
  starting transfers between devices  29.9 us (8%)
  local copies, waits for them, and re-layouts  21.4 us (5%)
  other arithmetic  8.24 us (2%)
    ppermute x1, waiting for transfers between devices, on_device(): edge_recv = lax.ppermute(edge_send, 'layer', across)  108 us
    ppermute x6, waiting for transfers between devices, shifted(): return [value] + [lax.ppermute(value, 'col', pairs) for pairs in moves]  63.1 us
    pallas_call x2, Pallas kernels, sweep_chunk(): pl.pallas_call(functools.partial(sweep_kernel, nt, first, count), out_sha...  34.8 us
    ppermute x1, waiting for transfers between devices, on_device(): received.append(lax.ppermute(sends[-1], 'layer', across))  27.6 us
    pallas_call x2, Pallas kernels, update_chunk(): pl.pallas_call(functools.partial(update_kernel, first, slab, rows // bloc...  26 us
    pallas_call x1, Pallas kernels, window_matrices(): pl.pallas_call(functools.partial(matrices_kernel, nt, group, shards), out...  16.5 us
    ppermute x1, waiting for transfers between devices, summed(): away = lax.ppermute(home, 'row', ring)  11.5 us
    ppermute x1, waiting for transfers between devices, summed(): home = home + lax.ppermute(away, 'row', ring)  11.1 us
  transfers between devices with their start and end apart: 33, of which 11 were waited for; matrix products, arithmetic and copies ran while one was open for 6% of the time, Pallas kernels for 15%

commit v1 on v0

v1 whole, which is shorter than its diff:
```python
import functools

import jax
import jax.numpy as jnp
from jax import lax
from jax.experimental import pallas as pl
from jax.experimental.pallas import tpu as pltpu
from jax.sharding import PartitionSpec as P


WIN = 256
HALF = 128
LANE = 128
F32 = jnp.float32
BF16 = jnp.bfloat16


def split(value):
    high = value.astype(BF16)
    return high, (value - high.astype(F32)).astype(BF16)


def dot(a, b):
    return jnp.dot(a, b, preferred_element_type=F32)


def product(a_high, a_low, b):
    b_high, b_low = split(b)
    return dot(a_high, b_high) + (dot(a_high, b_low) + dot(a_low, b_high))


def window_matrix(vec_t, fac_t):
    rows = lax.broadcasted_iota(jnp.int32, fac_t.shape, 0)
    cols = lax.broadcasted_iota(jnp.int32, fac_t.shape, 1)
    upper = jnp.where(rows >= cols, fac_t, 0.0).T
    up_high, up_low = split(upper)
    scaled = product(up_high, up_low, vec_t)
    v_high, v_low = split(vec_t.T)
    return product(v_high, v_low, scaled)


def params(*names, limit=None):
    return pltpu.CompilerParams(dimension_semantics=names, vmem_limit_bytes=limit)


def size_of(*shapes):
    total = 0
    for shape, kind in shapes:
        count = jnp.dtype(kind).itemsize
        for length in shape:
            count *= length
        total += count
    return total + 3 * 2**20


def cost(flops, size):
    return pl.CostEstimate(flops=flops, bytes_accessed=size, transcendentals=0)


def fill(place, sources, parts, store, sems):
    count = len(sources)

    def each(visit):
        for side in range(2):
            for i, (source, valid) in enumerate(sources):
                ref = parts[side * count + i]
                size = ref.shape[0]
                tile = place[1] if side == 0 else 1 - place[1]
                at = pl.ds(pl.multiple_of(source * size, 8), size)

                @pl.when(valid)
                def _():
                    visit(pltpu.make_async_copy(ref, store.at[tile, at, :], sems.at[side, i]))

    each(lambda copy: copy.start())
    each(lambda copy: copy.wait())


def shifted_sources(z, shards):
    return [(lax.rem(z - s + shards, shards), z >= 0) for s in range(shards)]


def line_sources(z, shards):
    found = [(z, z >= 0)]
    for s in range(1, shards):
        found.append((jnp.maximum(z - s, 0), z >= s))
    for s in range(1, shards):
        found.append((jnp.minimum(z + s, shards - 1), z + s < shards))
    return found


def edge_matrices_kernel(shards, place, *refs):
    high, low, edges, sems = refs[2 * shards :]

    @pl.when(pl.program_id(0) == 0)
    def _():
        fill(place, shifted_sources(place[2], shards), refs, edges, sems)

    base = pl.program_id(0) * 5 * HALF

    def edge(side, start, size):
        return edges[side, :, pl.ds(pl.multiple_of(base + start, LANE), size)]

    above = window_matrix(edge(1, 0, WIN), edge(1, 3 * HALF, HALF))
    below = window_matrix(edge(0, 0, WIN), edge(0, 3 * HALF, HALF))
    middle = jnp.concatenate([edge(1, WIN, HALF), edge(0, WIN, HALF)], axis=1)
    middle = window_matrix(middle, edge(0, 4 * HALF, HALF))
    for i, value in enumerate((above, below, middle)):
        h, l = split(value)
        high[0, i] = h
        low[0, i] = l


def edge_matrices(place, own, mate):
    shards = len(own)
    house, width = shards * own[0].shape[0], own[0].shape[1]
    edge = pl.BlockSpec((1, 3, WIN, WIN), lambda k, place: (k, 0, 0, 0))
    shape = jax.ShapeDtypeStruct((3, 3, WIN, WIN), BF16)
    return pl.pallas_call(
        functools.partial(edge_matrices_kernel, shards),
        out_shape=(shape, shape),
        grid_spec=pltpu.PrefetchScalarGridSpec(
            num_scalar_prefetch=1,
            grid=(3,),
            in_specs=[pl.BlockSpec(memory_space=pl.ANY)] * (2 * shards),
            out_specs=[edge, edge],
            scratch_shapes=[
                pltpu.VMEM((2, house, width), F32),
                pltpu.SemaphoreType.DMA((2, shards)),
            ],
        ),
        compiler_params=params("arbitrary", limit=16 * 2**20),
        cost_estimate=cost(2 * 10**9, 4 * 2**20),
        name="edge_matrices",
    )(place, *own, *mate)


def matrices_kernel(nt, group, shards, place, *refs):
    panel, panel_mate, mats, vecs, sems = refs[2 * (2 * shards - 1) :]
    rows = nt * WIN

    @pl.when(pl.program_id(0) == 0)
    def _():
        fill(place, line_sources(place[2], shards), refs, vecs, sems)

    def piece(tile, start, size):
        return vecs[tile, :, pl.ds(pl.multiple_of(start, LANE), size)]

    for i in range(group):
        k = pl.program_id(0) * group + i
        tile = k // nt
        at = k % nt
        factor = piece(tile, 2 * rows + at * HALF, HALF)
        h, l = split(window_matrix(piece(tile, at * WIN, WIN), factor))
        mats[i, 0] = h
        mats[i, 1] = l
        before = jnp.maximum(k * WIN - HALF, 0)
        left = piece(before // rows, rows + before % rows, HALF)
        right = piece(tile, rows + at * WIN, HALF)
        factor = piece(tile, 2 * rows + rows // 2 + at * HALF, HALF)
        h, l = split(window_matrix(jnp.concatenate([left, right], axis=1), factor))
        mats[i, 2] = h
        mats[i, 3] = l
        block = slice(i * WIN, (i + 1) * WIN)
        mine = tile == place[1]
        h, l = split(jnp.where(mine, panel[block, :], panel_mate[block, :]).T)
        mats[i, 4] = h
        mats[i, 5] = l


def window_matrices(place, own, mate, panel, panel_mate, nt):
    shards = (len(own) + 1) // 2
    nw = 2 * nt
    group = 2
    arrays = (*own, *mate)
    in_specs = [pl.BlockSpec(memory_space=pl.ANY)] * len(arrays)
    width = panel.shape[1]
    panel_spec = pl.BlockSpec((group * WIN, width), lambda k, place: (k % (nt // group), 0))
    house = shards * own[0].shape[0]
    return pl.pallas_call(
        functools.partial(matrices_kernel, nt, group, shards),
        out_shape=jax.ShapeDtypeStruct((nw, 6, WIN, WIN), BF16),
        grid_spec=pltpu.PrefetchScalarGridSpec(
            num_scalar_prefetch=1,
            grid=(nw // group,),
            in_specs=[*in_specs, panel_spec, panel_spec],
            out_specs=pl.BlockSpec((group, 6, WIN, WIN), lambda k, place: (k, 0, 0, 0)),
            scratch_shapes=[
                pltpu.VMEM((2, house, own[0].shape[1]), F32),
                pltpu.SemaphoreType.DMA((2, len(own))),
            ],
        ),
        compiler_params=params("arbitrary", limit=32 * 2**20),
        cost_estimate=cost(6 * 10**9, 24 * 2**20),
        name="window_matrices",
    )(place, *arrays, panel, panel_mate)


def edge_kernel(high, low, above, below, out):
    a = above[0]
    b = below[0]
    a = a - product(high[0, 0], low[0, 0], a)
    b = b - product(high[0, 1], low[0, 1], b)
    m = jnp.concatenate([a[HALF:], b[:HALF]], axis=0)
    m = m - product(high[0, 2], low[0, 2], m)
    out[0, 0, :HALF] = a[:HALF]
    out[0, 0, HALF:] = m[:HALF]
    out[0, 1, :HALF] = m[HALF:]
    out[0, 1, HALF:] = b[HALF:]


def sweep_edges(high, low, above, below):
    width = above.shape[2]
    mats = pl.BlockSpec((1, 3, WIN, WIN), lambda b, i: (b, 0, 0, 0))
    step = min(width, 2 * LANE)
    data = pl.BlockSpec((1, WIN, step), lambda b, i: (b, 0, i))
    return pl.pallas_call(
        edge_kernel,
        out_shape=jax.ShapeDtypeStruct((3, 2, WIN, width), F32),
        grid=(3, width // step),
        in_specs=[mats, mats, data, data],
        out_specs=pl.BlockSpec((1, 2, WIN, step), lambda b, i: (b, 0, 0, i)),
        compiler_params=params("arbitrary", "arbitrary", limit=16 * 2**20),
        cost_estimate=cost(6 * 10**9, 8 * 2**20),
        name="sweep_edges",
    )(high, low, above, below)


def stacked_product(mats, k, at, data):
    high, low = split(data)
    left = jnp.concatenate([mats[k, at], mats[k, at], mats[k, at + 1]], axis=1)
    return dot(left, jnp.concatenate([high, low, high], axis=0))


def sweep_kernel(nt, own, recv_spec, cuts, place, *refs):
    total = sum(len(lengths) for _, _, lengths in recv_spec)
    data, own_edge, recv_edge, mats_in = refs[:4]
    recv = refs[4 : 4 + total]
    keep, send = refs[4 + total : 6 + total]
    parts = refs[6 + total : 6 + total + len(cuts)]
    data_buf, mats, data_sems, mats_sems, out_sems = refs[6 + total + len(cuts) :]
    nw = 2 * nt
    x, core = place[0], place[1]

    def spot(base, step, mine):
        where = base + (x if mine else 1 - x) * step if step else base
        return where if isinstance(where, int) else pl.multiple_of(where, LANE)

    def block(k):
        return pl.ds(pl.multiple_of(k * WIN, WIN), WIN)

    def mats_copy(k):
        return pltpu.make_async_copy(mats_in.at[k], mats.at[k], mats_sems.at[k])

    def own_copies(k):
        return [
            pltpu.make_async_copy(
                data.at[block(x * nw + k), pl.ds(first * LANE, count * LANE)],
                data_buf.at[block(k), pl.ds(spot(base, step, True), count * LANE)],
                data_sems.at[k, i],
            )
            for i, (first, count, base, step) in enumerate(own)
        ]

    def recv_copy(k, i, at, offset):
        _, place_at, _ = recv_spec[i]
        return pltpu.make_async_copy(
            recv[at].at[block(k - 1 - offset), :],
            data_buf.at[block(k), pl.ds(spot(*place_at, False), LANE)],
            data_sems.at[k, len(own) + i],
        )

    def each_recv(visit):
        at = 0
        for i, (_, _, lengths) in enumerate(recv_spec):
            offset = 0
            for length in lengths:
                visit(i, at, offset, length)
                offset += length
                at += 1

    def start_inner(k):
        for copy in own_copies(k):
            copy.start()
        mats_copy(k).start()

        def one(i, at, offset, length):
            if length == nw - 2:
                recv_copy(k, i, at, offset).start()
            else:
                inside = jnp.logical_and(k - 1 >= offset, k - 1 < offset + length)

                @pl.when(inside)
                def _():
                    recv_copy(k, i, at, offset).start()

        each_recv(one)

    def wait_inner(k):
        for copy in own_copies(k):
            copy.wait()
        mats_copy(k).wait()

        def one(i, at, offset, length):
            if offset == 0:
                recv_copy(k, i, at, k - 1).wait()

        each_recv(one)

    def edge_copies(end):
        k = end * (nw - 1)
        found = [
            pltpu.make_async_copy(
                own_edge.at[x + end, 1 - end, :, pl.ds(first * LANE, count * LANE)],
                data_buf.at[block(k), pl.ds(spot(base, step, True), count * LANE)],
                data_sems.at[k, i],
            )
            for i, (first, count, base, step) in enumerate(own)
        ]
        for i, (first, place_at, _) in enumerate(recv_spec):
            found.append(
                pltpu.make_async_copy(
                    recv_edge.at[end, :, pl.ds(first * LANE, LANE)],
                    data_buf.at[block(k), pl.ds(spot(*place_at, False), LANE)],
                    data_sems.at[k, len(own) + i],
                )
            )
        return found

    def out_copy(ref, b, tile):
        return pltpu.make_async_copy(
            data_buf.at[block(b), :], ref.at[block(b - tile * nt), :], out_sems.at[b]
        )

    for copy in edge_copies(0):
        copy.start()
    mats_copy(0).start()

    @pl.loop(1, nw - 1)
    def _(k):
        start_inner(k)

    for copy in edge_copies(1):
        copy.start()
    mats_copy(nw - 1).start()
    for part in parts:
        part[...] = jnp.zeros_like(part)
    for copy in edge_copies(0):
        copy.wait()
    mats_copy(0).wait()

    def stage(t, one, two, three):
        if one:
            wait_inner(t)
        elif two and three:
            if isinstance(t, int) and t == nw - 1:
                for copy in edge_copies(1):
                    copy.wait()
                mats_copy(nw - 1).wait()
        r1 = block(t)
        r2 = pl.ds(pl.multiple_of((t - 1) * WIN - HALF, HALF), WIN)
        b = t - 3
        r3 = block(b)
        d1 = data_buf[r1, :] if one else None
        d2 = data_buf[r2, :] if two else None
        d3 = data_buf[r3, :] if three else None
        if one:
            d1 = d1 - stacked_product(mats, t, 0, d1)
        if two:
            d2 = d2 - stacked_product(mats, t - 1, 2, d2)
        if three:
            d3 = stacked_product(mats, b, 4, d3)
        if one:
            data_buf[r1, :] = d1
        if two:
            data_buf[r2, :] = d2
        if three:
            for part, (low, high) in zip(parts, cuts):
                part[...] += d3[:, low:high]
            mine = b // nt == core

            @pl.when(mine)
            def _():
                out_copy(keep, b, core).start()

            @pl.when(jnp.logical_not(mine))
            def _():
                out_copy(send, b, 1 - core).start()

    stage(1, True, False, False)
    stage(2, True, True, False)

    @pl.loop(3, nw - 1)
    def _(t):
        stage(t, True, True, True)

    stage(nw - 1, False, True, True)
    stage(nw, False, True, True)
    stage(nw + 1, False, False, True)
    stage(nw + 2, False, False, True)

    @pl.loop(0, nt)
    def _(i):
        out_copy(keep, core * nt + i, core).wait()
        out_copy(send, (1 - core) * nt + i, 1 - core).wait()


def sweep_chunk(place, own, recv, cuts, data, own_edge, recv_edge, mats, house, nt):
    nw = 2 * nt
    cols = cuts[-1][1]
    hbm = pl.BlockSpec(memory_space=pl.ANY)
    shape = jax.ShapeDtypeStruct((nt * WIN, cols), F32)
    recv_spec = tuple(
        (first, at, tuple(part.shape[0] // WIN for part in piece)) for first, at, piece in recv
    )
    parts = [part for _, _, piece in recv for part in piece]
    widths = [high - low for low, high in cuts]
    return pl.pallas_call(
        functools.partial(sweep_kernel, nt, own, recv_spec, cuts),
        out_shape=(shape, shape, *[jax.ShapeDtypeStruct((house, width), F32) for width in widths]),
        grid_spec=pltpu.PrefetchScalarGridSpec(
            num_scalar_prefetch=1,
            grid=(1,),
            in_specs=[hbm] * (4 + len(parts)),
            out_specs=[
                hbm,
                hbm,
                *[pl.BlockSpec((house, width), lambda i, place: (0, 0)) for width in widths],
            ],
            scratch_shapes=[
                pltpu.VMEM((nw * WIN, cols), F32),
                pltpu.VMEM((nw, 6, WIN, WIN), BF16),
                pltpu.SemaphoreType.DMA((nw, len(own) + len(recv))),
                pltpu.SemaphoreType.DMA((nw,)),
                pltpu.SemaphoreType.DMA((nw,)),
            ],
        ),
        compiler_params=params("arbitrary", limit=52 * 2**20),
        cost_estimate=cost(nw * 9 * 2 * WIN**2 * cols, nw * WIN * (8 * cols + 6 * WIN)),
    )(place, data, own_edge, recv_edge, mats, *parts)


def update_kernel(first, slab, resident, aliased, place, *refs):
    refs = refs[1:] if aliased else refs
    sides = 2
    factor, *proj = refs[:5]
    panel, keep, mate, out, wh, wl, rows_buf, panel_buf, in_sems, out_sems = refs[5:]
    height = panel.shape[0]
    width = proj[0].shape[1]
    steps = height // WIN

    def block(k):
        return pl.ds(pl.multiple_of(k * WIN, WIN), WIN)

    def in_copies(k):
        return [
            pltpu.make_async_copy(panel.at[block(k), :], panel_buf.at[block(k), :], in_sems.at[0, k]),
            pltpu.make_async_copy(keep.at[block(k), :], rows_buf.at[0, block(k), :], in_sems.at[1, k]),
            pltpu.make_async_copy(mate.at[block(k), :], rows_buf.at[1, block(k), :], in_sems.at[2, k]),
        ]

    def out_copies(k):
        found = []
        for at in range(2):
            core = place[1] if at == 0 else 1 - place[1]
            for i in range(sides):
                x = i
                column = pl.multiple_of((2 * x + core) * slab + first * LANE, LANE)
                found.append(
                    pltpu.make_async_copy(
                        rows_buf.at[at, block(k), i * width : (i + 1) * width],
                        out.at[block(k), pl.ds(column, width)],
                        out_sems.at[sides * at + i, k],
                    )
                )
        return found

    if not resident:

        @pl.loop(0, steps)
        def _(k):
            for copy in in_copies(k):
                copy.start()

    r = lax.broadcasted_iota(jnp.int32, factor.shape, 0)
    c = lax.broadcasted_iota(jnp.int32, factor.shape, 1)
    uh, ul = split(jnp.where(r <= c, factor[...], 0.0))
    for i, source in enumerate(proj):
        lanes = slice((i % sides) * width, (i % sides + 1) * width)
        h, l = split(product(uh, ul, source[...]))
        wh[i // sides, :, lanes] = h
        wl[i // sides, :, lanes] = l

    @pl.loop(0, steps)
    def _(k):
        if not resident:
            for copy in in_copies(k):
                copy.wait()
        source = panel if resident else panel_buf
        ph, pl_ = split(source[block(k), :])
        left = jnp.concatenate([ph, ph, pl_], axis=1)
        for at in range(2):
            right = jnp.concatenate([wh[at], wl[at], wh[at]], axis=0)
            value = (keep, mate)[at][block(k), :] if resident else rows_buf[at, block(k), :]
            rows_buf[at, block(k), :] = value - dot(left, right)
        for copy in out_copies(k):
            copy.start()

    @pl.loop(0, steps)
    def _(k):
        for copy in out_copies(k):
            copy.wait()


def update_chunk(place, first, out, factor, proj, panel, keep, mate, slab, resident):
    rows, width = panel.shape
    cols = keep.shape[1]
    steps = rows // WIN
    aliased = out is not None
    hbm = pl.BlockSpec(memory_space=pl.ANY)
    vmem = pl.BlockSpec(memory_space=pltpu.VMEM)
    in_specs = [vmem] * 5 + ([vmem] * 3 if resident else [hbm] * 3)
    sources = [panel, keep, mate]
    if resident:
        sources = [pltpu.with_memory_space_constraint(value, pltpu.VMEM) for value in sources]
    args = [factor, *proj, *sources]
    if aliased:
        in_specs = [hbm] + in_specs
        args = [out] + args
    return pl.pallas_call(
        functools.partial(update_kernel, first, slab, resident, aliased),
        out_shape=jax.ShapeDtypeStruct((rows, 4 * slab), F32),
        grid_spec=pltpu.PrefetchScalarGridSpec(
            num_scalar_prefetch=1,
            grid=(),
            in_specs=in_specs,
            out_specs=hbm,
            scratch_shapes=[
                pltpu.VMEM((2, width, cols), BF16),
                pltpu.VMEM((2, width, cols), BF16),
                pltpu.VMEM((2, rows, cols), F32),
                pltpu.VMEM((8, width) if resident else (rows, width), F32),
                pltpu.SemaphoreType.DMA((3, steps)),
                pltpu.SemaphoreType.DMA((4, steps)),
            ],
        ),
        input_output_aliases={1: 0} if aliased else {},
        compiler_params=pltpu.CompilerParams(
            vmem_limit_bytes=size_of(
                ((2, rows, cols), F32), ((rows, width), F32), ((8 * width, cols), F32), ((4 * width, width), F32)
            )
        ),
        cost_estimate=cost(6 * rows * width * 2 * cols, 4 * rows * (4 * cols + width)),
    )(place, *args)


def on_device(rows_n, cols_n, eigvecs, v1, v2, f1, f2, panel, panel_factor):
    layer = lax.axis_index("layer")
    row = lax.axis_index("row")
    z = lax.axis_index("col")
    x, core = layer // 2, layer % 2
    place = jnp.stack([x, core, z]).astype(jnp.int32)
    across = [(0, 2), (2, 0), (1, 3), (3, 1)]
    mates = [(0, 1), (1, 0), (2, 3), (3, 2)]
    height, slab = eigvecs.shape
    chip = height // 2
    nt = chip // WIN // 2
    chunks = slab // LANE
    house = panel.shape[1]

    def shifted(value):
        moves = [[(i, (i + s) % cols_n) for i in range(cols_n)] for s in range(1, cols_n)]
        return [value] + [lax.ppermute(value, "col", pairs) for pairs in moves]

    t1, t2, g1, g2 = v1.T, v2.T, f1.T, f2.T
    blank = jnp.zeros((t1.shape[0], HALF), F32)
    top = jnp.concatenate([t1[:, :WIN], t2[:, :HALF], g1[:, :HALF], g2[:, :HALF]], axis=1)
    bottom = jnp.concatenate([t1[:, -WIN:], t2[:, -HALF:], g1[:, -HALF:], blank], axis=1)
    mine = jnp.where(core == 0, top, bottom)
    peer = lax.ppermute(mine, "layer", across)

    received = []
    inner = chip - 2 * WIN

    def send_chunk(source, j):
        top_row = (1 - x) * chip + WIN
        part = max(inner // WIN // 7, 1) * WIN if j == 0 else inner
        part = inner // WIN // 2 * WIN if j == chunks - 1 else part
        sizes = [part, inner - part] if part < inner else [part]
        piece = []
        for i, size in enumerate(sizes):
            value = lax.dynamic_slice(source, (top_row + i * part, j * LANE), (size, LANE))
            source, value = lax.optimization_barrier((source, value))
            piece.append(lax.ppermute(value, "layer", across))
        received.append(piece)
        return source

    source = send_chunk(eigvecs, 0)
    inner_end, outer_end = jnp.where(x == core, mine, peer), jnp.where(x == core, peer, mine)
    pairs = []
    for r in range(rows_n - 1):
        for l in range(4):
            low, high = r * 4 + l, (r + 1) * 4 + l
            pairs.append((high, low) if l % 2 == 0 else (low, high))
    beyond = lax.ppermute(inner_end, ("row", "layer"), pairs)
    edges = jnp.concatenate(
        [
            jnp.where(core == 0, inner_end, beyond),
            outer_end,
            jnp.where(core == 0, beyond, inner_end),
        ],
        axis=1,
    )
    own_edges = shifted(edges)
    stacked = jnp.concatenate([t1, t2, g1, g2], axis=1)
    right = [stacked]
    left = [stacked]
    for _ in range(1, cols_n):
        right.append(lax.ppermute(right[-1], "col", [(i, i + 1) for i in range(cols_n - 1)]))
        left.append(lax.ppermute(left[-1], "col", [(i + 1, i) for i in range(cols_n - 1)]))
    own = right + left[1:]
    source, edges = lax.optimization_barrier((source, edges))
    for j in range(1, chunks):
        source = send_chunk(source, j)
    halo_above = lax.ppermute(source[-WIN:], "row", [(r, r + 1) for r in range(rows_n - 1)])
    halo_below = lax.ppermute(source[:WIN], "row", [(r + 1, r) for r in range(rows_n - 1)])
    panel_mate = lax.ppermute(panel, "layer", mates)
    mate = [lax.ppermute(value, "layer", mates) for value in own]
    mate_edges = [lax.ppermute(value, "layer", mates) for value in own_edges]

    bh, bl = edge_matrices(place, own_edges, mate_edges)
    above = jnp.stack([halo_above, eigvecs[chip - WIN : chip], eigvecs[-WIN:]])
    below = jnp.stack([eigvecs[:WIN], eigvecs[chip : chip + WIN], halo_below])
    swept = sweep_edges(bh, bl, above, below)
    edge_send = jnp.stack(
        [
            lax.dynamic_index_in_dim(swept[:, 1], 1 - x, 0, keepdims=False),
            lax.dynamic_index_in_dim(swept[:, 0], 2 - x, 0, keepdims=False),
        ]
    )
    edge_recv = lax.ppermute(edge_send, "layer", across)
    mats = window_matrices(place, own, mate, panel, panel_mate, nt)

    def swept_chunk(first, count):
        span = count * LANE
        recv = [(first + i, (i * LANE, span), received[first + i]) for i in range(count)]
        return sweep_chunk(
            place, ((first, count, 0, span),), recv, ((0, span), (span, 2 * span)), eigvecs, swept,
            edge_recv, mats, house, nt,
        )

    ring = [(r, (r + 1) % rows_n) for r in range(rows_n)]

    def over_rows(value):
        moving = value
        for _ in range(rows_n - 1):
            moving = lax.ppermute(moving, "row", ring)
            value = value + moving
        return value

    def over_x(value):
        return value + lax.ppermute(value, "layer", across)

    def summed(parts):
        if rows_n != 2:
            return [over_rows(over_x(part)) for part in parts]
        first = row == 0
        away = jnp.where(first, parts[1], parts[0])
        home = jnp.where(first, parts[0], parts[1])
        home = over_x(home + lax.ppermute(away, "row", ring))
        away = lax.ppermute(home, "row", ring)
        return [jnp.where(first, home, away), jnp.where(first, away, home)]

    def summed_last(parts):
        one = over_x(parts[0])
        two = over_rows(parts[1])
        return [over_rows(one), over_x(two)]

    def updated(first, out, keep, other, totals):
        mates_totals = [lax.ppermute(total, "layer", mates) for total in totals]
        return update_chunk(
            place, first, out, panel_factor, (*totals, *mates_totals), panel, keep, other, slab,
            False,
        )

    out = None
    for name, first, count in groups(chunks):
        keep, send, *parts = swept_chunk(first, count)
        other = lax.ppermute(send, "layer", mates)
        totals = summed_last(parts) if name == "b" else summed(parts)
        out = updated(first, out, keep, other, totals)
    return out


def groups(chunks):
    if chunks < 3:
        return [("a", 0, chunks - 1), ("b", chunks - 1, 1)]
    return [("a", 0, chunks - 2), ("c", chunks - 2, 1), ("b", chunks - 1, 1)]


def solution(mesh):
    in_specs = (
        P("row", ("col", "layer")),
        P(("row", "layer"), "col"),
        P(("row", "layer"), "col"),
        P(("row", "layer"), "col"),
        P(("row", "layer"), "col"),
        P(("row", "layer"), None),
        P(),
    )

    def body(*args):
        return on_device(mesh.shape["row"], mesh.shape["col"], *args)

    return jax.shard_map(
        body,
        mesh=mesh,
        in_specs=in_specs,
        out_specs=P(("row", "layer"), "col"),
        check_vma=False,
    )
```

time: 392 us -> 337 us (0.86)
  waiting for transfers between devices: 239 us -> 171 us
  starting transfers between devices: 29.9 us -> 53.1 us
  Pallas kernels: 92.2 us -> 82 us
  local copies, waits for them, and re-layouts: 21.4 us -> 28.2 us
  other arithmetic: 8.24 us -> 1.99 us
    ppermute x1, waiting for transfers between devices: 108 us -> 0.01 us  [on_device(): edge_recv = lax.ppermute(edge_send, 'layer', across)]
    ppermute x14 -> x31, waiting for transfers between devices: 53.4 us -> 159 us  [the longest x6 110 us: send_chunk(): piece.append(lax.ppermute(value, 'layer', across))]
    ppermute x6 -> x3, waiting for transfers between devices: 63.1 us -> 6.87 us  [shifted(): return [value] + [lax.ppermute(value, 'col', pairs) for pairs in moves]]
    ppermute x14 -> x31, starting transfers between devices: 13 us -> 39.8 us  [the longest x3 15.4 us: on_device(): lax.ppermute(right[-1], 'col', [(i, i + 1) for i in range(cols_n - 1)])]
    ppermute x1 -> x2, waiting for transfers between devices: 11.5 us -> 1.49 us  [summed(): away = lax.ppermute(home, 'row', ring)]
    ppermute x6 -> x3, starting transfers between devices: 8.69 us -> 5.17 us  [shifted(): return [value] + [lax.ppermute(value, 'col', pairs) for pairs in moves]]
    dynamic_slice x4 -> x6, local copies, waits for them, and re-layouts: 11.1 us -> 14.5 us  [send_chunk(): lax.dynamic_slice(source, (top_row + i * part, j * LANE), (size, LANE))]
    pallas_call x4 -> x6, Pallas kernels: 60.8 us -> 57.6 us  [the longest x3 37.8 us: sweep_chunk(): pl.pallas_call(functools.partial(sweep_kernel, nt, own, recv_spec, cuts),...]
  transfers between devices with their start and end apart: 33 -> 51, of which waited for: 11 -> 21; matrix products, arithmetic and copies ran while one was open for 6% -> 6% of each run, Pallas kernels for 15% -> 23%
where the time goes in v1:
time: 337 us
  waiting for transfers between devices  171 us (51%)
  Pallas kernels  82 us (24%)
  starting transfers between devices  53.1 us (16%)
  local copies, waits for them, and re-layouts  28.2 us (8%)
    ppermute x6, waiting for transfers between devices, send_chunk(): piece.append(lax.ppermute(value, 'layer', across))  110 us
    pallas_call x3, Pallas kernels, sweep_chunk(): pl.pallas_call(functools.partial(sweep_kernel, nt, own, recv_spec, cuts),...  37.8 us
    ppermute x3, waiting for transfers between devices, on_device(): lax.ppermute(left[-1], 'col', [(i + 1, i) for i in range(cols_n - 1)])  23.2 us
    pallas_call x3, Pallas kernels, update_chunk(): pl.pallas_call(functools.partial(update_kernel, first, slab, resident, al...  19.8 us
    ppermute x3, starting transfers between devices, on_device(): lax.ppermute(right[-1], 'col', [(i, i + 1) for i in range(cols_n - 1)])  15.4 us
    dynamic_slice x6, local copies, waits for them, and re-layouts, send_chunk(): lax.dynamic_slice(source, (top_row + i * part, j * LANE), (size, LANE))  14.5 us
    pallas_call x1, Pallas kernels, window_matrices(): pl.pallas_call(functools.partial(matrices_kernel, nt, group, shards), out...  12.9 us
    ppermute x2, waiting for transfers between devices, summed(): home = over_x(home + lax.ppermute(away, 'row', ring))  10 us
  transfers between devices with their start and end apart: 51, of which 21 were waited for; matrix products, arithmetic and copies ran while one was open for 6% of the time, Pallas kernels for 23%

profile of v1, /device:TPU:0, one launch (start us, length us, event | category | flops | bytes accessed | tf_op | source)
XLA Modules:
  0.0 336.6 jit_solution(2564841582542849005)
XLA Ops:
  0.0 0.7 slice.63
  0.7 0.8 fusion.2
  1.5 0.8 fusion.3
  2.3 3.0 collective-permute-start
  5.3 1.7 constant_dynamic-slice_fusion.1
  7.0 0.8 collective-permute-done
  7.8 1.3 collective-permute-start.1
  9.1 2.7 constant_dynamic-slice_fusion
  11.8 2.4 collective-permute-done.1
  14.3 4.2 %collective-permute-start.4 = (f32[32,1920]{1,0:T(8,128)S(1)}, f32[32,1920]{1,0:T(8,128)S(1)}, u32[]{:S(2)}, u32[]{:S(2)}) collective-permute-start(f32[32,1920]{1,0:T(8,128)S(1)} %pad_maximum_fusion.4.refs_0_), channel_id=1, source_target_pairs={{0,12},{4,0},{8,4},{12,8},{1,13},{5,1},{9,5},{13,9},{2,14},{6,2},{... | collective-permute-start | bytes 737288 | tf_op jit(solution)/shard_map/ppermute | solution.py:573
  18.4 1.0 collective-permute-start.2
  19.4 2.8 constant_dynamic-slice_fusion.4
  22.3 2.9 constant_dynamic-slice_fusion.5
  25.2 2.2 constant_dynamic-slice_fusion.3
  27.4 2.3 constant_dynamic-slice_fusion.2
  29.6 2.1 fusion
  31.7 1.3 collective-permute-start.10
  33.1 6.9 %collective-permute-done.3.refs_2_ = f32[32,1920]{1,0:T(8,128)S(1)} collective-permute-done((f32[32,1920]{1,0:T(8,128)S(1)}, f32[32,1920]{1,0:T(8,128)S(1)}, u32[]{:S(2)}, u32[]{:S(2)}) %collective-permute-start.3) | collective-permute-done | bytes 245792 | tf_op jit(solution)/shard_map/ppermute | solution.py:573
  40.6 0.8 copy-done.19
  41.3 1.3 collective-permute-start.15
  43.3 5.4 %collective-permute-start.12 = (f32[32,6144]{1,0:T(8,128)S(1)}, f32[32,6144]{1,0:T(8,128)}, u32[]{:S(2)}, u32[]{:S(2)}) collective-permute-start(f32[32,6144]{1,0:T(8,128)S(1)} %pad_maximum_fusion.3.refs_0_), channel_id=1, source_target_pairs={{0,4},{4,8},{8,12},{1,5},{5,9},{9,13},{2,6},{6,10},{10,14},{3,7},{... | collective-permute-start | bytes 2359304 | tf_op jit(solution)/shard_map/ppermute | solution.py:619
  49.5 3.0 collective-permute-start.9
  52.5 10.3 %collective-permute-done.15.refs_4_ = f32[32,6144]{1,0:T(8,128)} collective-permute-done((f32[32,6144]{1,0:T(8,128)S(1)}, f32[32,6144]{1,0:T(8,128)}, u32[]{:S(2)}, u32[]{:S(2)}) %collective-permute-start.15) | collective-permute-done | bytes 786464 | tf_op jit(solution)/shard_map/ppermute | solution.py:620
  62.9 1.3 collective-permute-start.16
  64.7 5.4 %collective-permute-start.13 = (f32[32,6144]{1,0:T(8,128)}, f32[32,6144]{1,0:T(8,128)}, u32[]{:S(2)}, u32[]{:S(2)}) collective-permute-start(f32[32,6144]{1,0:T(8,128)} %collective-permute-done.12.refs_1_), channel_id=1, source_target_pairs={{0,4},{4,8},{8,12},{1,5},{5,9},{9,13},{2,6},{6,10},{10,14},{3,7},{... | collective-permute-start | bytes 2359304 | tf_op jit(solution)/shard_map/ppermute | solution.py:619
  70.3 1.8 slice_bitcast_fusion.1
  72.3 6.3 %edge_matrices.1 = (bf16[3,3,256,256]{3,2,1,0:T(8,128)(2,1)S(1)}, bf16[3,3,256,256]{3,2,1,0:T(8,128)(2,1)S(1)}) custom-call(s32[3]{0:T(128)S(1)} %pad_add_fusion.place, f32[32,1920]{1,0:T(8,128)S(1)} %pad_maximum_fusion.4.refs_0_, f32[32,1920]{1,0:T(8,128)S(1)} %copy-done.18, f32[32,1920]{1,0:T(8,128)S(1)} %copy-done.16, f32[32,1920]{1,0:T(8,128)S(1)} %copy-done.14, ...), custom_call_target="tpu_custom_call" | custom-call | flops 2000000000 | bytes 4194304 | tf_op jit(solution)/shard_map/edge_matrices/pallas_call | solution.py:119
  78.7 5.5 %collective-permute-done.16.refs_5_ = f32[32,6144]{1,0:T(8,128)} collective-permute-done((f32[32,6144]{1,0:T(8,128)}, f32[32,6144]{1,0:T(8,128)}, u32[]{:S(2)}, u32[]{:S(2)}) %collective-permute-start.16) | collective-permute-done | bytes 786464 | tf_op jit(solution)/shard_map/ppermute | solution.py:620
  84.4 1.3 pad_maximum_fusion.above
  86.0 1.5 collective-permute-start.28
  87.5 1.3 collective-permute-start.17
  89.1 1.3 copy-done.7
  90.4 4.6 %collective-permute-start.14 = (f32[32,6144]{1,0:T(8,128)}, f32[32,6144]{1,0:T(8,128)S(1)}, u32[]{:S(2)}, u32[]{:S(2)}) collective-permute-start(f32[32,6144]{1,0:T(8,128)} %collective-permute-done.13.refs_2_), channel_id=1, source_target_pairs={{0,4},{4,8},{8,12},{1,5},{5,9},{9,13},{2,6},{6,10},{10,14},{3,7},{... | collective-permute-start | bytes 2359304 | tf_op jit(solution)/shard_map/ppermute | solution.py:619
  95.0 5.1 %sweep_edges.1.refs_1_ = f32[3,2,256,512]{3,2,1,0:T(8,128)S(1)} custom-call(bf16[3,3,256,256]{3,2,1,0:T(8,128)(2,1)S(1)} %get-tuple-element.32.high, bf16[3,3,256,256]{3,2,1,0:T(8,128)(2,1)S(1)} %get-tuple-element.33.low, f32[3,256,512]{2,1,0:T(8,128)S(1)} %pad_maximum_fusion.above, f32[3,256,512]{2,1,0:T(8,128)S(1)} %pad_maximum_fusion.1.below), custom_call_target="tpu_custom_call" | custom-call | flops 6000000000 | bytes 8388608 | tf_op jit(solution)/shard_map/sweep_edges/pallas_call | solution.py:217
  102.0 7.3 %collective-permute-done.17.refs_6_ = f32[32,6144]{1,0:T(8,128)S(1)} collective-permute-done((f32[32,6144]{1,0:T(8,128)}, f32[32,6144]{1,0:T(8,128)S(1)}, u32[]{:S(2)}, u32[]{:S(2)}) %collective-permute-start.17) | collective-permute-done | bytes 786464 | tf_op jit(solution)/shard_map/ppermute | solution.py:620
  109.3 3.2 collective-permute-done.14.refs_3_
  113.5 1.3 collective-permute-start.26
  115.5 12.9 %window_matrices.1.refs_3_ = bf16[16,6,256,256]{3,2,1,0:T(8,128)(2,1)} custom-call(s32[3]{0:T(128)S(1)} %pad_add_fusion.place, f32[32,6144]{1,0:T(8,128)S(1)} %copy-done.5, f32[32,6144]{1,0:T(8,128)} %collective-permute-done.12.refs_1_, f32[32,6144]{1,0:T(8,128)} %collective-permute-done.13.refs_2_, f32[32,6144]{1,0:T(8,128)S(1)} %collective-permute-done.14.refs_3_, ...), custom_call_target="tpu_custom_call" | custom-call | flops 6000000000 | bytes 25165824 | tf_op jit(solution)/shard_map/window_matrices/pallas_call | solution.py:180
  128.5 62.2 %collective-permute-done.26.refs_4_ = f32[512,128]{1,0:T(8,128)S(1)} collective-permute-done((f32[512,128]{1,0:T(8,128)S(1)}, f32[512,128]{1,0:T(8,128)S(1)}, u32[]{:S(2)}, u32[]{:S(2)}) %collective-permute-start.26) | collective-permute-done | bytes 262176 | tf_op jit(solution)/shard_map/ppermute | solution.py:594
  190.7 1.1 copy-done.26
  191.9 16.0 %shard_map.73 = (f32[2048,512]{1,0:T(8,128)}, f32[2048,512]{1,0:T(8,128)}, f32[256,256]{1,0:T(8,128)S(1)}, f32[256,256]{1,0:T(8,128)S(1)}) custom-call(s32[3]{0:T(128)S(1)} %pad_add_fusion.place, f32[8192,512]{1,0:T(8,128)} %refs_0_.7, f32[3,2,256,512]{3,2,1,0:T(8,128)} %copy-done, f32[2,256,512]{2,1,0:T(8,128)S(1)} %collective-permute-done.11.refs_2_, ...), custom_call_target="tpu_custom_call" | custom-call | flops 9663676416 | bytes 23068672 | tf_op jit(solution)/shard_map/pallas_call | solution.py:418
  208.6 1.5 collective-permute-start.43
  210.6 19.5 %collective-permute-done.35.refs_4_ = f32[3584,128]{1,0:T(8,128)} collective-permute-done((f32[3584,128]{1,0:T(8,128)}, f32[3584,128]{1,0:T(8,128)}, u32[]{:S(2)}, u32[]{:S(2)}) %collective-permute-start.35) | collective-permute-done | bytes 1835040 | tf_op jit(solution)/shard_map/ppermute | solution.py:594
  230.1 10.8 %shard_map.75 = (f32[2048,256]{1,0:T(8,128)}, f32[2048,256]{1,0:T(8,128)}, f32[256,128]{1,0:T(8,128)S(1)}, f32[256,128]{1,0:T(8,128)S(1)}) custom-call(s32[3]{0:T(128)S(1)} %pad_add_fusion.place, f32[8192,512]{1,0:T(8,128)} %refs_0_.7, f32[3,2,256,512]{3,2,1,0:T(8,128)} %copy-done, f32[2,256,512]{2,1,0:T(8,128)S(1)} %collective-permute-done.11.refs_2_, ...), custom_call_target="tpu_custom_call" | custom-call | flops 4831838208 | bytes 14680064 | tf_op jit(solution)/shard_map/pallas_call | solution.py:418
  241.1 8.7 %collective-permute-done.43.refs_5_ = f32[1792,128]{1,0:T(8,128)} collective-permute-done((f32[1792,128]{1,0:T(8,128)}, f32[1792,128]{1,0:T(8,128)}, u32[]{:S(2)}, u32[]{:S(2)}) %collective-permute-start.43) | collective-permute-done | bytes 917536 | tf_op jit(solution)/shard_map/ppermute | solution.py:594
  249.8 19.2 %collective-permute-done.42.refs_4_ = f32[1792,128]{1,0:T(8,128)} collective-permute-done((f32[1792,128]{1,0:T(8,128)}, f32[1792,128]{1,0:T(8,128)}, u32[]{:S(2)}, u32[]{:S(2)}) %collective-permute-start.42) | collective-permute-done | bytes 917536 | tf_op jit(solution)/shard_map/ppermute | solution.py:594
  269.0 11.0 %shard_map.77 = (f32[2048,256]{1,0:T(8,128)}, f32[2048,256]{1,0:T(8,128)}, f32[256,128]{1,0:T(8,128)S(1)}, f32[256,128]{1,0:T(8,128)S(1)}) custom-call(s32[3]{0:T(128)S(1)} %pad_add_fusion.place, f32[8192,512]{1,0:T(8,128)} %refs_0_.7, f32[3,2,256,512]{3,2,1,0:T(8,128)} %copy-done, f32[2,256,512]{2,1,0:T(8,128)} %copy-done.2, ...), custom_call_target="tpu_custom_call" | custom-call | flops 4831838208 | bytes 14680064 | tf_op jit(solution)/shard_map/pallas_call | solution.py:418
  280.4 1.5 collective-permute-start.44
  281.9 6.9 %collective-permute-done.29 = f32[256,256]{1,0:T(8,128)S(1)} collective-permute-done((f32[256,256]{1,0:T(8,128)S(1)}, f32[256,256]{1,0:T(8,128)S(1)}, u32[]{:S(2)}, u32[]{:S(2)}) %collective-permute-start.29) | collective-permute-done | bytes 262176 | tf_op jit(solution)/shard_map/ppermute | solution.py:670
  289.2 1.6 collective-permute-start.30
  290.8 3.1 collective-permute-done.36
  294.2 2.6 collective-permute-done.30
  296.8 1.5 collective-permute-start.37
  298.8 1.3 collective-permute-start.31
  300.2 1.6 collective-permute-done.37
  301.8 1.7 collective-permute-start.45
  303.6 4.2 %collective-permute-done.45 = f32[256,128]{1,0:T(8,128)S(1)} collective-permute-done((f32[256,128]{1,0:T(8,128)S(1)}, f32[256,128]{1,0:T(8,128)S(1)}, u32[]{:S(2)}, u32[]{:S(2)}) %collective-permute-start.45) | collective-permute-done | bytes 131104 | tf_op jit(solution)/shard_map/ppermute | solution.py:657
  307.8 1.5 collective-permute-start.47
  310.0 2.7 collective-permute-done.47
  312.8 1.5 collective-permute-done.38
  314.9 0.9 collective-permute-done.32.refs_3_
  316.3 7.9 %shard_map.74.refs_0_ = f32[2048,2048]{1,0:T(8,128)} custom-call(s32[3]{0:T(128)S(1)} %pad_add_fusion.place, f32[256,256]{1,0:T(8,128)S(1)} %copy-done.6, f32[256,256]{1,0:T(8,128)S(1)} %get-tuple-element.68.refs_1_, f32[256,256]{1,0:T(8,128)S(1)} %get-tuple-element.67.refs_2_, f32[256,256]{1,0:T(8,128)S(1)} %collective-permute-done.32.refs_3_, ...), custom_call_target="tpu_custom_call" | custom-call | flops 3221225472 | bytes 18874368 | tf_op jit(solution)/shard_map/pallas_call | solution.py:530
  324.5 5.9 %shard_map.76.refs_0_ = f32[2048,2048]{1,0:T(8,128)} custom-call(s32[3]{0:T(128)S(1)} %pad_add_fusion.place, f32[2048,2048]{1,0:T(8,128)} %shard_map.74.refs_0_, f32[256,256]{1,0:T(8,128)S(1)} %copy-done.6, f32[256,128]{1,0:T(8,128)S(1)} %get-tuple-element.70.refs_2_, f32[256,128]{1,0:T(8,128)S(1)} %get-tuple-element.69.refs_3_, ...), custom_call_target="tpu_custom_call", output_to_operand_aliasing={{}: (1, {})} | custom-call | flops 1610612736 | bytes 10485760 | tf_op jit(solution)/shard_map/pallas_call | solution.py:530
  330.5 5.9 %shard_map.78 = f32[2048,2048]{1,0:T(8,128)} custom-call(s32[3]{0:T(128)S(1)} %pad_add_fusion.place, f32[2048,2048]{1,0:T(8,128)} %shard_map.76.refs_0_, f32[256,256]{1,0:T(8,128)S(1)} %copy-done.6, f32[256,128]{1,0:T(8,128)S(1)} %add.86.refs_2_, f32[256,128]{1,0:T(8,128)S(1)} %add.88.refs_3_, ...), custom_call_target="tpu_custom_call", output_to_operand_aliasing={{}: (1, {})} | custom-call | flops 1610612736 | bytes 10485760 | tf_op jit(solution)/shard_map/pallas_call | solution.py:530
  (154 shorter events, 12.6 us)
Async XLA Ops:
  2.3 5.5 %collective-permute-start = (f32[32,640]{1,0:T(8,128)S(1)}, f32[32,640]{1,0:T(8,128)S(1)}, u32[]{:S(2)}, u32[]{:S(2)}) collective-permute-start(f32[32,640]{1,0:T(8,128)S(1)} %maximum_select_fusion), channel_id=1, source_target_pairs={{0,2},{2,0},{1,3},{3,1},{4,6},{6,4},{5,7},{7,5},{8,10},{10,8},{9,1... | collective-permute-start | bytes 245768 | tf_op jit(solution)/shard_map/ppermute | solution.py:580
  5.3 83.8 %collective-permute-start.25 = (f32[2048,256]{1,0:T(8,128)}, f32[2048,256]{1,0:T(8,128)S(1)}, u32[]{:S(2)}, u32[]{:S(2)}) collective-permute-start(f32[2048,256]{1,0:T(8,128)} %refs_6_.3), channel_id=1, source_target_pairs={{0,1},{1,0},{2,3},{3,2},{4,5},{5,4},{6,7},{7,6},{8,9},{9,8},{10,11... | collective-permute-start | bytes 6291464 | tf_op jit(solution)/shard_map/ppermute | solution.py:627
  7.8 6.3 %collective-permute-start.1 = (f32[32,640]{1,0:T(8,128)S(1)}, f32[32,640]{1,0:T(8,128)S(1)}, u32[]{:S(2)}, u32[]{:S(2)}) collective-permute-start(f32[32,640]{1,0:T(8,128)S(1)} %get-tuple-element.78), channel_id=1, source_target_pairs={{16,0},{1,17},{18,2},{3,19},{20,4},{5,21},{22,6},{7,23},{24,8},{9,... | collective-permute-start | bytes 245768 | tf_op jit(solution)/shard_map/ppermute | solution.py:605
  14.2 17.5 %collective-permute-start.5 = (f32[32,1920]{1,0:T(8,128)S(1)}, f32[32,1920]{1,0:T(8,128)S(1)}, u32[]{:S(2)}, u32[]{:S(2)}) collective-permute-start(f32[32,1920]{1,0:T(8,128)S(1)} %pad_maximum_fusion.4.refs_0_), channel_id=1, source_target_pairs={{0,1},{1,0},{2,3},{3,2},{4,5},{5,4},{6,7},{7,6},{8,9},{9,8},{10,11... | collective-permute-start | bytes 737288 | tf_op jit(solution)/shard_map/ppermute | solution.py:629
  14.3 18.7 %collective-permute-start.4 = (f32[32,1920]{1,0:T(8,128)S(1)}, f32[32,1920]{1,0:T(8,128)S(1)}, u32[]{:S(2)}, u32[]{:S(2)}) collective-permute-start(f32[32,1920]{1,0:T(8,128)S(1)} %pad_maximum_fusion.4.refs_0_), channel_id=1, source_target_pairs={{0,12},{4,0},{8,4},{12,8},{1,13},{5,1},{9,5},{13,9},{2,14},{6,2},{... | collective-permute-start | bytes 737288 | tf_op jit(solution)/shard_map/ppermute | solution.py:573
  18.4 21.5 %collective-permute-start.3 = (f32[32,1920]{1,0:T(8,128)S(1)}, f32[32,1920]{1,0:T(8,128)S(1)}, u32[]{:S(2)}, u32[]{:S(2)}) collective-permute-start(f32[32,1920]{1,0:T(8,128)S(1)} %pad_maximum_fusion.4.refs_0_), channel_id=1, source_target_pairs={{0,8},{4,12},{8,0},{12,4},{1,9},{5,13},{9,1},{13,5},{2,10},{6,14},... | collective-permute-start | bytes 737288 | tf_op jit(solution)/shard_map/ppermute | solution.py:573
  18.4 21.5 %collective-permute-start.2 = (f32[32,1920]{1,0:T(8,128)S(1)}, f32[32,1920]{1,0:T(8,128)S(1)}, u32[]{:S(2)}, u32[]{:S(2)}) collective-permute-start(f32[32,1920]{1,0:T(8,128)S(1)} %pad_maximum_fusion.4.refs_0_), channel_id=1, source_target_pairs={{0,4},{4,8},{8,12},{12,0},{1,5},{5,9},{9,13},{13,1},{2,6},{6,10},{... | collective-permute-start | bytes 737288 | tf_op jit(solution)/shard_map/ppermute | solution.py:573
  27.3 13.1 %copy-start.31 = (f32[2048,32]{0,1:T(8,128)S(1)}, f32[2048,32]{0,1:T(8,128)}, u32[]{:S(2)}) copy-start(f32[2048,32]{0,1:T(8,128)} %param.9) | copy-start | bytes 786436
  27.3 13.1 %copy-start.33 = (f32[1024,32]{0,1:T(8,128)S(1)}, f32[1024,32]{0,1:T(8,128)}, u32[]{:S(2)}) copy-start(f32[1024,32]{0,1:T(8,128)} %param.10) | copy-start | bytes 393220
  27.3 13.1 %copy-start.34 = (f32[1024,32]{0,1:T(8,128)S(1)}, f32[1024,32]{0,1:T(8,128)}, u32[]{:S(2)}) copy-start(f32[1024,32]{0,1:T(8,128)} %param.11) | copy-start | bytes 393220
  31.7 17.8 %collective-permute-start.10 = (f32[256,512]{1,0:T(8,128)S(1)}, f32[256,512]{1,0:T(8,128)S(1)}, u32[]{:S(2)}, u32[]{:S(2)}) collective-permute-start(f32[256,512]{1,0:T(8,128)S(1)} %get-tuple-element.63), channel_id=1, source_target_pairs={{16,0},{17,1},{18,2},{19,3},{20,4},{21,5},{22,6},{23,7},{24,8},{25... | collective-permute-start | bytes 1572872 | tf_op jit(solution)/shard_map/ppermute | solution.py:626
  33.0 29.9 %copy-start.13 = (f32[32,1920]{1,0:T(8,128)}, f32[32,1920]{1,0:T(8,128)S(1)}, u32[]{:S(2)}) copy-start(f32[32,1920]{1,0:T(8,128)S(1)} %collective-permute-done.4.refs_3_) | copy-start | bytes 737284
  33.0 7.6 %collective-permute-start.8 = (f32[32,1920]{1,0:T(8,128)S(1)}, f32[32,1920]{1,0:T(8,128)S(1)}, u32[]{:S(2)}, u32[]{:S(2)}) collective-permute-start(f32[32,1920]{1,0:T(8,128)S(1)} %collective-permute-done.4.refs_3_), channel_id=1, source_target_pairs={{0,1},{1,0},{2,3},{3,2},{4,5},{5,4},{6,7},{7,6},{8,9},{9,8},{10,11... | collective-permute-start | bytes 737288 | tf_op jit(solution)/shard_map/ppermute | solution.py:629
  39.9 22.9 %copy-start.15 = (f32[32,1920]{1,0:T(8,128)}, f32[32,1920]{1,0:T(8,128)S(1)}, u32[]{:S(2)}) copy-start(f32[32,1920]{1,0:T(8,128)S(1)} %collective-permute-done.3.refs_2_) | copy-start | bytes 737284
  39.9 2.7 collective-permute-start.7
  39.9 22.9 %copy-start.17 = (f32[32,1920]{1,0:T(8,128)}, f32[32,1920]{1,0:T(8,128)S(1)}, u32[]{:S(2)}) copy-start(f32[32,1920]{1,0:T(8,128)S(1)} %collective-permute-done.2.refs_1_) | copy-start | bytes 737284
  40.0 8.8 %collective-permute-start.6 = (f32[32,1920]{1,0:T(8,128)S(1)}, f32[32,1920]{1,0:T(8,128)S(1)}, u32[]{:S(2)}, u32[]{:S(2)}) collective-permute-start(f32[32,1920]{1,0:T(8,128)S(1)} %collective-permute-done.2.refs_1_), channel_id=1, source_target_pairs={{0,1},{1,0},{2,3},{3,2},{4,5},{5,4},{6,7},{7,6},{8,9},{9,8},{10,11... | collective-permute-start | bytes 737288 | tf_op jit(solution)/shard_map/ppermute | solution.py:629
  40.5 31.6 %copy-start.4 = (f32[32,6144]{1,0:T(8,128)}, f32[32,6144]{1,0:T(8,128)S(1)}, u32[]{:S(2)}) copy-start(f32[32,6144]{1,0:T(8,128)S(1)} %pad_maximum_fusion.3.refs_0_) | copy-start | bytes 2359300
  41.3 21.5 %collective-permute-start.15 = (f32[32,6144]{1,0:T(8,128)S(1)}, f32[32,6144]{1,0:T(8,128)}, u32[]{:S(2)}, u32[]{:S(2)}) collective-permute-start(f32[32,6144]{1,0:T(8,128)S(1)} %pad_maximum_fusion.3.refs_0_), channel_id=1, source_target_pairs={{4,0},{8,4},{12,8},{5,1},{9,5},{13,9},{6,2},{10,6},{14,10},{7,3},{... | collective-permute-start | bytes 2359304 | tf_op jit(solution)/shard_map/ppermute | solution.py:620
  43.3 21.3 %collective-permute-start.12 = (f32[32,6144]{1,0:T(8,128)S(1)}, f32[32,6144]{1,0:T(8,128)}, u32[]{:S(2)}, u32[]{:S(2)}) collective-permute-start(f32[32,6144]{1,0:T(8,128)S(1)} %pad_maximum_fusion.3.refs_0_), channel_id=1, source_target_pairs={{0,4},{4,8},{8,12},{1,5},{5,9},{9,13},{2,6},{6,10},{10,14},{3,7},{... | collective-permute-start | bytes 2359304 | tf_op jit(solution)/shard_map/ppermute | solution.py:619
  49.5 15.3 %collective-permute-start.18 = (f32[32,6144]{1,0:T(8,128)S(1)}, f32[32,6144]{1,0:T(8,128)}, u32[]{:S(2)}, u32[]{:S(2)}) collective-permute-start(f32[32,6144]{1,0:T(8,128)S(1)} %pad_maximum_fusion.3.refs_0_), channel_id=1, source_target_pairs={{0,1},{1,0},{2,3},{3,2},{4,5},{5,4},{6,7},{7,6},{8,9},{9,8},{10,11... | collective-permute-start | bytes 2359304 | tf_op jit(solution)/shard_map/ppermute | solution.py:628
  49.5 13.4 %copy-start.28 = (f32[256,512]{1,0:T(8,128)}, f32[256,512]{1,0:T(8,128)S(1)}, u32[]{:S(2)}) copy-start(f32[256,512]{1,0:T(8,128)S(1)} %collective-permute-done.10) | copy-start | bytes 1572868
  49.5 14.7 %collective-permute-start.9 = (f32[256,512]{1,0:T(8,128)}, f32[256,512]{1,0:T(8,128)}, u32[]{:S(2)}, u32[]{:S(2)}) collective-permute-start(f32[256,512]{1,0:T(8,128)} %get-tuple-element.64), channel_id=1, source_target_pairs={{0,16},{1,17},{2,18},{3,19},{4,20},{5,21},{6,22},{7,23},{8,24},{9,... | collective-permute-start | bytes 1572872 | tf_op jit(solution)/shard_map/ppermute | solution.py:625
  62.9 21.4 %collective-permute-start.16 = (f32[32,6144]{1,0:T(8,128)}, f32[32,6144]{1,0:T(8,128)}, u32[]{:S(2)}, u32[]{:S(2)}) collective-permute-start(f32[32,6144]{1,0:T(8,128)} %collective-permute-done.15.refs_4_), channel_id=1, source_target_pairs={{4,0},{8,4},{12,8},{5,1},{9,5},{13,9},{6,2},{10,6},{14,10},{7,3},{... | collective-permute-start | bytes 2359304 | tf_op jit(solution)/shard_map/ppermute | solution.py:620
  64.2 21.5 %collective-permute-start.22 = (f32[32,6144]{1,0:T(8,128)}, f32[32,6144]{1,0:T(8,128)}, u32[]{:S(2)}, u32[]{:S(2)}) collective-permute-start(f32[32,6144]{1,0:T(8,128)} %collective-permute-done.15.refs_4_), channel_id=1, source_target_pairs={{0,1},{1,0},{2,3},{3,2},{4,5},{5,4},{6,7},{7,6},{8,9},{9,8},{10,11... | collective-permute-start | bytes 2359304 | tf_op jit(solution)/shard_map/ppermute | solution.py:628
  64.6 22.9 %collective-permute-start.19 = (f32[32,6144]{1,0:T(8,128)}, f32[32,6144]{1,0:T(8,128)}, u32[]{:S(2)}, u32[]{:S(2)}) collective-permute-start(f32[32,6144]{1,0:T(8,128)} %collective-permute-done.12.refs_1_), channel_id=1, source_target_pairs={{0,1},{1,0},{2,3},{3,2},{4,5},{5,4},{6,7},{7,6},{8,9},{9,8},{10,11... | collective-permute-start | bytes 2359304 | tf_op jit(solution)/shard_map/ppermute | solution.py:628
  64.7 24.1 %collective-permute-start.13 = (f32[32,6144]{1,0:T(8,128)}, f32[32,6144]{1,0:T(8,128)}, u32[]{:S(2)}, u32[]{:S(2)}) collective-permute-start(f32[32,6144]{1,0:T(8,128)} %collective-permute-done.12.refs_1_), channel_id=1, source_target_pairs={{0,4},{4,8},{8,12},{1,5},{5,9},{9,13},{2,6},{6,10},{10,14},{3,7},{... | collective-permute-start | bytes 2359304 | tf_op jit(solution)/shard_map/ppermute | solution.py:619
  84.2 15.9 %collective-permute-start.23 = (f32[32,6144]{1,0:T(8,128)}, f32[32,6144]{1,0:T(8,128)S(1)}, u32[]{:S(2)}, u32[]{:S(2)}) collective-permute-start(f32[32,6144]{1,0:T(8,128)} %collective-permute-done.16.refs_5_), channel_id=1, source_target_pairs={{0,1},{1,0},{2,3},{3,2},{4,5},{5,4},{6,7},{7,6},{8,9},{9,8},{10,11... | collective-permute-start | bytes 2359304 | tf_op jit(solution)/shard_map/ppermute | solution.py:628
  86.0 105.8 %collective-permute-start.28 = (f32[3584,128]{1,0:T(8,128)S(1)}, f32[3584,128]{1,0:T(8,128)}, u32[]{:S(2)}, u32[]{:S(2)}) collective-permute-start(f32[3584,128]{1,0:T(8,128)S(1)} %copy-done.25), channel_id=1, source_target_pairs={{0,2},{2,0},{1,3},{3,1},{4,6},{6,4},{5,7},{7,5},{8,10},{10,8},{9,1... | collective-permute-start | bytes 5505032 | tf_op jit(solution)/shard_map/ppermute | solution.py:594
  87.5 21.8 %collective-permute-start.17 = (f32[32,6144]{1,0:T(8,128)}, f32[32,6144]{1,0:T(8,128)S(1)}, u32[]{:S(2)}, u32[]{:S(2)}) collective-permute-start(f32[32,6144]{1,0:T(8,128)} %collective-permute-done.16.refs_5_), channel_id=1, source_target_pairs={{4,0},{8,4},{12,8},{5,1},{9,5},{13,9},{6,2},{10,6},{14,10},{7,3},{... | collective-permute-start | bytes 2359304 | tf_op jit(solution)/shard_map/ppermute | solution.py:620
  88.8 23.9 %collective-permute-start.20 = (f32[32,6144]{1,0:T(8,128)}, f32[32,6144]{1,0:T(8,128)S(1)}, u32[]{:S(2)}, u32[]{:S(2)}) collective-permute-start(f32[32,6144]{1,0:T(8,128)} %collective-permute-done.13.refs_2_), channel_id=1, source_target_pairs={{0,1},{1,0},{2,3},{3,2},{4,5},{5,4},{6,7},{7,6},{8,9},{9,8},{10,11... | collective-permute-start | bytes 2359304 | tf_op jit(solution)/shard_map/ppermute | solution.py:628
  90.4 22.1 %collective-permute-start.14 = (f32[32,6144]{1,0:T(8,128)}, f32[32,6144]{1,0:T(8,128)S(1)}, u32[]{:S(2)}, u32[]{:S(2)}) collective-permute-start(f32[32,6144]{1,0:T(8,128)} %collective-permute-done.13.refs_2_), channel_id=1, source_target_pairs={{0,4},{4,8},{8,12},{1,5},{5,9},{9,13},{2,6},{6,10},{10,14},{3,7},{... | collective-permute-start | bytes 2359304 | tf_op jit(solution)/shard_map/ppermute | solution.py:619
  100.1 90.6 %collective-permute-start.27 = (f32[3072,128]{1,0:T(8,128)S(1)}, f32[3072,128]{1,0:T(8,128)S(1)}, u32[]{:S(2)}, u32[]{:S(2)}) collective-permute-start(f32[3072,128]{1,0:T(8,128)S(1)} %copy-done.27), channel_id=1, source_target_pairs={{0,2},{2,0},{1,3},{3,1},{4,6},{6,4},{5,7},{7,5},{8,10},{10,8},{9,1... | collective-permute-start | bytes 4718600 | tf_op jit(solution)/shard_map/ppermute | solution.py:594
  100.7 14.8 %copy-start.8 = (f32[2048,256]{1,0:T(8,128)S(1)}, f32[2048,256]{1,0:T(8,128)}, u32[]{:S(2)}) copy-start(f32[2048,256]{1,0:T(8,128)} %copy-done.7) | copy-start | bytes 6291460
  109.3 4.1 %collective-permute-start.24 = (f32[32,6144]{1,0:T(8,128)S(1)}, f32[32,6144]{1,0:T(8,128)S(1)}, u32[]{:S(2)}, u32[]{:S(2)}) collective-permute-start(f32[32,6144]{1,0:T(8,128)S(1)} %collective-permute-done.17.refs_6_), channel_id=1, source_target_pairs={{0,1},{1,0},{2,3},{3,2},{4,5},{5,4},{6,7},{7,6},{8,9},{9,8},{10,11... | collective-permute-start | bytes 2359304 | tf_op jit(solution)/shard_map/ppermute | solution.py:628
  112.5 2.3 collective-permute-start.21
  112.7 78.0 %collective-permute-start.11 = (f32[2,256,512]{2,1,0:T(8,128)S(1)}, f32[2,256,512]{2,1,0:T(8,128)S(1)}, u32[]{:S(2)}, u32[]{:S(2)}) collective-permute-start(f32[2,256,512]{2,1,0:T(8,128)S(1)} %pad_maximum_fusion.2), channel_id=1, source_target_pairs={{0,2},{2,0},{1,3},{3,1},{4,6},{6,4},{5,7},{7,5},{8,10},{10,8},{9,1... | collective-permute-start | bytes 3145736 | tf_op jit(solution)/shard_map/ppermute | solution.py:641
  113.5 77.2 %collective-permute-start.26 = (f32[512,128]{1,0:T(8,128)S(1)}, f32[512,128]{1,0:T(8,128)S(1)}, u32[]{:S(2)}, u32[]{:S(2)}) collective-permute-start(f32[512,128]{1,0:T(8,128)S(1)} %copy-done.32), channel_id=1, source_target_pairs={{0,2},{2,0},{1,3},{3,1},{4,6},{6,4},{5,7},{7,5},{8,10},{10,8},{9,1... | collective-permute-start | bytes 786440 | tf_op jit(solution)/shard_map/ppermute | solution.py:594
  114.8 115.3 %collective-permute-start.35 = (f32[3584,128]{1,0:T(8,128)}, f32[3584,128]{1,0:T(8,128)}, u32[]{:S(2)}, u32[]{:S(2)}) collective-permute-start(f32[3584,128]{1,0:T(8,128)} %constant_dynamic-slice_fusion.5), channel_id=1, source_target_pairs={{0,2},{2,0},{1,3},{3,1},{4,6},{6,4},{5,7},{7,5},{8,10},{10,8},{9,1... | collective-permute-start | bytes 5505032 | tf_op jit(solution)/shard_map/ppermute | solution.py:594
  191.9 38.3 %copy-start.2 = (f32[2,256,512]{2,1,0:T(8,128)}, f32[2,256,512]{2,1,0:T(8,128)S(1)}, u32[]{:S(2)}) copy-start(f32[2,256,512]{2,1,0:T(8,128)S(1)} %collective-permute-done.11.refs_2_) | copy-start | bytes 3145732
  208.6 107.3 %collective-permute-start.34 = (f32[2048,512]{1,0:T(8,128)}, f32[2048,512]{1,0:T(8,128)}, u32[]{:S(2)}, u32[]{:S(2)}) collective-permute-start(f32[2048,512]{1,0:T(8,128)} %get-tuple-element.47), channel_id=1, source_target_pairs={{0,1},{1,0},{2,3},{3,2},{4,5},{5,4},{6,7},{7,6},{8,9},{9,8},{10,11... | collective-permute-start | bytes 12582920 | tf_op jit(solution)/shard_map/ppermute | solution.py:689
  208.6 41.2 %collective-permute-start.43 = (f32[1792,128]{1,0:T(8,128)}, f32[1792,128]{1,0:T(8,128)}, u32[]{:S(2)}, u32[]{:S(2)}) collective-permute-start(f32[1792,128]{1,0:T(8,128)} %constant_dynamic-slice_fusion.2), channel_id=1, source_target_pairs={{0,2},{2,0},{1,3},{3,1},{4,6},{6,4},{5,7},{7,5},{8,10},{10,8},{9,1... | collective-permute-start | bytes 2752520 | tf_op jit(solution)/shard_map/ppermute | solution.py:594
  210.1 58.9 %collective-permute-start.42 = (f32[1792,128]{1,0:T(8,128)}, f32[1792,128]{1,0:T(8,128)}, u32[]{:S(2)}, u32[]{:S(2)}) collective-permute-start(f32[1792,128]{1,0:T(8,128)} %constant_dynamic-slice_fusion.3), channel_id=1, source_target_pairs={{0,2},{2,0},{1,3},{3,1},{4,6},{6,4},{5,7},{7,5},{8,10},{10,8},{9,1... | collective-permute-start | bytes 2752520 | tf_op jit(solution)/shard_map/ppermute | solution.py:594
  241.0 39.0 %copy-start.12 = (f32[256,256]{1,0:T(8,128)S(1)}, f32[256,256]{1,0:T(8,128)}, u32[]{:S(2)}) copy-start(f32[256,256]{1,0:T(8,128)} %copy-done.11) | copy-start | bytes 786436
  241.0 83.5 %collective-permute-start.41 = (f32[2048,256]{1,0:T(8,128)}, f32[2048,256]{1,0:T(8,128)S(1)}, u32[]{:S(2)}, u32[]{:S(2)}) collective-permute-start(f32[2048,256]{1,0:T(8,128)} %get-tuple-element.52), channel_id=1, source_target_pairs={{0,1},{1,0},{2,3},{3,2},{4,5},{5,4},{6,7},{7,6},{8,9},{9,8},{10,11... | collective-permute-start | bytes 6291464 | tf_op jit(solution)/shard_map/ppermute | solution.py:689
  279.9 50.5 %collective-permute-start.50 = (f32[2048,256]{1,0:T(8,128)}, f32[2048,256]{1,0:T(8,128)S(1)}, u32[]{:S(2)}, u32[]{:S(2)}) collective-permute-start(f32[2048,256]{1,0:T(8,128)} %get-tuple-element.58), channel_id=1, source_target_pairs={{0,1},{1,0},{2,3},{3,2},{4,5},{5,4},{6,7},{7,6},{8,9},{9,8},{10,11... | collective-permute-start | bytes 6291464 | tf_op jit(solution)/shard_map/ppermute | solution.py:689
  280.1 8.8 %collective-permute-start.29 = (f32[256,256]{1,0:T(8,128)S(1)}, f32[256,256]{1,0:T(8,128)S(1)}, u32[]{:S(2)}, u32[]{:S(2)}) collective-permute-start(f32[256,256]{1,0:T(8,128)S(1)} %broadcast_select_fusion.2), channel_id=1, source_target_pairs={{0,16},{16,0},{1,17},{17,1},{2,18},{18,2},{3,19},{19,3},{4,20},{20... | collective-permute-start | bytes 786440 | tf_op jit(solution)/shard_map/ppermute | solution.py:670
  280.4 8.8 %collective-permute-start.44 = (f32[256,128]{1,0:T(8,128)S(1)}, f32[256,128]{1,0:T(8,128)S(1)}, u32[]{:S(2)}, u32[]{:S(2)}) collective-permute-start(f32[256,128]{1,0:T(8,128)S(1)} %get-tuple-element.55), channel_id=1, source_target_pairs={{0,2},{2,0},{1,3},{3,1},{4,6},{6,4},{5,7},{7,5},{8,10},{10,8},{9,1... | collective-permute-start | bytes 393224 | tf_op jit(solution)/shard_map/ppermute | solution.py:662
  288.8 5.0 %collective-permute-start.36 = (f32[256,128]{1,0:T(8,128)S(1)}, f32[256,128]{1,0:T(8,128)S(1)}, u32[]{:S(2)}, u32[]{:S(2)}) collective-permute-start(f32[256,128]{1,0:T(8,128)S(1)} %broadcast_select_fusion.5), channel_id=1, source_target_pairs={{0,16},{16,0},{1,17},{17,1},{2,18},{18,2},{3,19},{19,3},{4,20},{20... | collective-permute-start | bytes 393224 | tf_op jit(solution)/shard_map/ppermute | solution.py:670
  289.2 7.6 %collective-permute-start.30 = (f32[256,256]{1,0:T(8,128)S(1)}, f32[256,256]{1,0:T(8,128)S(1)}, u32[]{:S(2)}, u32[]{:S(2)}) collective-permute-start(f32[256,256]{1,0:T(8,128)S(1)} %select_add_fusion), channel_id=1, source_target_pairs={{0,2},{2,0},{1,3},{3,1},{4,6},{6,4},{5,7},{7,5},{8,10},{10,8},{9,1... | collective-permute-start | bytes 786440 | tf_op jit(solution)/shard_map/ppermute | solution.py:662
  293.9 5.0 %collective-permute-start.46 = (f32[256,128]{1,0:T(8,128)S(1)}, f32[256,128]{1,0:T(8,128)S(1)}, u32[]{:S(2)}, u32[]{:S(2)}) collective-permute-start(f32[256,128]{1,0:T(8,128)S(1)} %get-tuple-element.56), channel_id=1, source_target_pairs={{0,16},{16,0},{1,17},{17,1},{2,18},{18,2},{3,19},{19,3},{4,20},{20... | collective-permute-start | bytes 393224 | tf_op jit(solution)/shard_map/ppermute | solution.py:657
  294.2 22.1 %copy-start.6 = (f32[256,256]{1,0:T(8,128)S(1)}, f32[256,256]{1,0:T(8,128)}, u32[]{:S(2)}) copy-start(f32[256,256]{1,0:T(8,128)} %refs_1_.3) | copy-start | bytes 786436
  296.8 5.0 %collective-permute-start.37 = (f32[256,128]{1,0:T(8,128)S(1)}, f32[256,128]{1,0:T(8,128)S(1)}, u32[]{:S(2)}, u32[]{:S(2)}) collective-permute-start(f32[256,128]{1,0:T(8,128)S(1)} %select_add_fusion.1), channel_id=1, source_target_pairs={{0,2},{2,0},{1,3},{3,1},{4,6},{6,4},{5,7},{7,5},{8,10},{10,8},{9,1... | collective-permute-start | bytes 393224 | tf_op jit(solution)/shard_map/ppermute | solution.py:662
  298.3 18.0 %copy-start.3 = (f32[2048,512]{1,0:T(8,128)S(1)}, f32[2048,512]{1,0:T(8,128)}, u32[]{:S(2)}) copy-start(f32[2048,512]{1,0:T(8,128)} %get-tuple-element.46.refs_6_) | copy-start | bytes 12582916
  298.8 10.4 %collective-permute-start.31 = (f32[256,256]{1,0:T(8,128)S(1)}, f32[256,256]{1,0:T(8,128)S(1)}, u32[]{:S(2)}, u32[]{:S(2)}) collective-permute-start(f32[256,256]{1,0:T(8,128)S(1)} %add.82), channel_id=1, source_target_pairs={{0,16},{16,0},{1,17},{17,1},{2,18},{18,2},{3,19},{19,3},{4,20},{20... | collective-permute-start | bytes 786440 | tf_op jit(solution)/shard_map/ppermute | solution.py:671
  301.8 6.0 %collective-permute-start.45 = (f32[256,128]{1,0:T(8,128)S(1)}, f32[256,128]{1,0:T(8,128)S(1)}, u32[]{:S(2)}, u32[]{:S(2)}) collective-permute-start(f32[256,128]{1,0:T(8,128)S(1)} %add.85), channel_id=1, source_target_pairs={{0,16},{16,0},{1,17},{17,1},{2,18},{18,2},{3,19},{19,3},{4,20},{20... | collective-permute-start | bytes 393224 | tf_op jit(solution)/shard_map/ppermute | solution.py:657
  307.8 5.0 %collective-permute-start.47 = (f32[256,128]{1,0:T(8,128)S(1)}, f32[256,128]{1,0:T(8,128)S(1)}, u32[]{:S(2)}, u32[]{:S(2)}) collective-permute-start(f32[256,128]{1,0:T(8,128)S(1)} %add.87), channel_id=1, source_target_pairs={{0,2},{2,0},{1,3},{3,1},{4,6},{6,4},{5,7},{7,5},{8,10},{10,8},{9,1... | collective-permute-start | bytes 393224 | tf_op jit(solution)/shard_map/ppermute | solution.py:662
  309.3 5.0 %collective-permute-start.38 = (f32[256,128]{1,0:T(8,128)S(1)}, f32[256,128]{1,0:T(8,128)S(1)}, u32[]{:S(2)}, u32[]{:S(2)}) collective-permute-start(f32[256,128]{1,0:T(8,128)S(1)} %add.84), channel_id=1, source_target_pairs={{0,16},{16,0},{1,17},{17,1},{2,18},{18,2},{3,19},{19,3},{4,20},{20... | collective-permute-start | bytes 393224 | tf_op jit(solution)/shard_map/ppermute | solution.py:671
  312.7 1.6 collective-permute-start.33
  314.2 1.5 collective-permute-start.32
  314.3 16.1 %collective-permute-start.48 = (f32[256,128]{1,0:T(8,128)S(1)}, f32[256,128]{1,0:T(8,128)S(1)}, u32[]{:S(2)}, u32[]{:S(2)}) collective-permute-start(f32[256,128]{1,0:T(8,128)S(1)} %add.86.refs_2_), channel_id=1, source_target_pairs={{0,1},{1,0},{2,3},{3,2},{4,5},{5,4},{6,7},{7,6},{8,9},{9,8},{10,11... | collective-permute-start | bytes 393224 | tf_op jit(solution)/shard_map/ppermute | solution.py:680
  315.8 8.5 %collective-permute-start.40 = (f32[256,128]{1,0:T(8,128)S(1)}, f32[256,128]{1,0:T(8,128)S(1)}, u32[]{:S(2)}, u32[]{:S(2)}) collective-permute-start(f32[256,128]{1,0:T(8,128)S(1)} %get-tuple-element.69.refs_3_), channel_id=1, source_target_pairs={{0,1},{1,0},{2,3},{3,2},{4,5},{5,4},{6,7},{7,6},{8,9},{9,8},{10,11... | collective-permute-start | bytes 393224 | tf_op jit(solution)/shard_map/ppermute | solution.py:680
  315.9 8.5 %collective-permute-start.39 = (f32[256,128]{1,0:T(8,128)S(1)}, f32[256,128]{1,0:T(8,128)S(1)}, u32[]{:S(2)}, u32[]{:S(2)}) collective-permute-start(f32[256,128]{1,0:T(8,128)S(1)} %get-tuple-element.70.refs_2_), channel_id=1, source_target_pairs={{0,1},{1,0},{2,3},{3,2},{4,5},{5,4},{6,7},{7,6},{8,9},{9,8},{10,11... | collective-permute-start | bytes 393224 | tf_op jit(solution)/shard_map/ppermute | solution.py:680
  324.3 6.2 %collective-permute-start.49 = (f32[256,128]{1,0:T(8,128)S(1)}, f32[256,128]{1,0:T(8,128)S(1)}, u32[]{:S(2)}, u32[]{:S(2)}) collective-permute-start(f32[256,128]{1,0:T(8,128)S(1)} %add.88.refs_3_), channel_id=1, source_target_pairs={{0,1},{1,0},{2,3},{3,2},{4,5},{5,4},{6,7},{7,6},{8,9},{9,8},{10,11... | collective-permute-start | bytes 393224 | tf_op jit(solution)/shard_map/ppermute | solution.py:680
  (22 other events, 71.7 us)
